TPU v7x, 256 devices: a whole 4x4x8 slice. The times are simulated.
256 devices in a mesh: seq: 32 (over x_lo, z, core), head: 8 (over y, x_hi).
Axes of the slice: x: 4 (x_hi: 2, x_lo: 2; x = x_hi * 2 + x_lo), y: 4, z: 8, core: 2. Of those that a mesh axis runs over, the one named last changes fastest.
Arguments:
- tokens: bfloat16 [16384, 4096], P('seq', 'head'), may hold values from -64 to 64
- norm_gain: float32 [4096], replicated, may hold values from 0.5 to 1.5
- w_query: bfloat16 [4096, 4096], P(None, 'head'), may hold values from -4 to 4
- w_key: bfloat16 [4096, 1024], P(None, 'head'), may hold values from -4 to 4
- w_value: bfloat16 [4096, 1024], P(None, 'head'), may hold values from -0.09375 to 0.09375
- w_output: bfloat16 [4096, 4096], P('head'), may hold values from -0.09375 to 0.09375
- widths: int32 [128], P('seq'), may hold values from 1 to 32
- dilation: int32 [128, 8], replicated, may hold values from 0 to 127, as said below
Outputs:
- layer_out: bfloat16 [16384, 4096], P('seq', 'head')
Inputs may be any that keep to these rules, and one draw needn't show every extreme that they name: `dilation`: the 8 entries of one row differ. Over the 4 aligned rows of one index of seq, all entries that fall into the blocks of one index of seq (ids k * 4 to k * 4 + 3) name the same block. Row i names blocks of the indices 0 to max(i // 4, 8) - 1 of seq only.
All inputs are finite; a program needn't handle non-finite values.
Results may differ from a plain program's by a relative error of at most 0.005.
Values may be sent and summed in bfloat16 or wider, within the bound.
No kernel may reach another device: no remote copies, remote signals or barrier semaphores. Data moves between devices by JAX's collectives and lax.ppermute only.
A program may use at most 128 MiB of HBM per device.

v0:
```python
import functools
import math

import jax
import jax.numpy as jnp
from jax import lax
from jax.experimental import pallas as pl
from jax.experimental.pallas import tpu as pltpu
from jax.sharding import Mesh
from jax.sharding import PartitionSpec as P

MODEL_WIDTH = 4096
HEAD_WIDTH = 128
BLOCK = 128
DILATION_COUNT = 8
ROWS = 512
HALF = 256
QB = 4
SEQ = ("seq_0", "seq_1", "seq_2")
HEAD = ("head_0", "head_1")
YS, XS, ZS = 4, 2, 8
EPSILON = 1e-05
NEGATIVE = -1e30
ROPE_BASE = 10000.0
SCORE_FACTOR = math.log2(math.e) / math.sqrt(HEAD_WIDTH)
GROUP = 4


def moved(x, axis, size, step):
    return lax.ppermute(x, axis, [(k, (k + step) % size) for k in range(size)])


def y_up(x):
    return moved(x, "head_0", YS, 1)


def y_down(x):
    return moved(x, "head_0", YS, -1)


def x_flip(x):
    return moved(x, "head_1", XS, 1)


def pair_flip(x):
    return moved(x, "seq_0", 2, 1)


def core_flip(x):
    return moved(x, "seq_2", 2, 1)


def gather_features(a):
    n = a.shape[0] // 2
    b = x_flip(a)
    u = y_up(a)
    d = y_down(a)
    ct = y_up(u[:n])
    cb = y_down(d[n:])
    bu = y_up(b)
    bd = y_down(b)
    et = x_flip(ct)
    eb = x_flip(cb)
    return (a, b, u, d, bu, bd), (ct, cb, et, eb)


FEATURE_FROM = ((0, 0), (0, 1), (-1, 0), (1, 0), (-1, 1), (1, 1), (2, 0), (2, 1))


def ring(x):
    pairs = []
    for z in range(ZS):
        pairs.append((2 * z, 2 * ((z + 1) % ZS)))
        pairs.append((2 * z + 1, 2 * ((z - 1) % ZS) + 1))
    return lax.ppermute(x, ("seq_1", "seq_2"), pairs)


def cat(*v):
    return jnp.concatenate(v, axis=0)


def gather_blocks(k):
    n = k.shape[0]
    k2 = cat(k, core_flip(k))
    b = pair_flip(k)
    r1 = ring(k2)
    b2 = cat(b, core_flip(b))
    r2 = ring(r1)
    rb1 = ring(b2)
    r3 = ring(r2)
    s1 = core_flip(cat(r1, r2))
    rb2 = ring(rb1)
    r4 = ring(r3[:n])
    f3 = pair_flip(r3)
    s2 = core_flip(cat(rb1, r3, r4))
    f4 = pair_flip(r4)
    s3 = core_flip(cat(rb2, f3, f4))
    return k2, b2, r1, r2, rb1, r3, r4, rb2, f3, f4, s1, s2, s3


PARTS_OF = {
    "k2": ((0, 0, 0), (0, 0, 1)),
    "b2": ((1, 0, 0), (1, 0, 1)),
    "r1": ((0, 1, 0), (0, 1, 1)),
    "r2": ((0, 2, 0), (0, 2, 1)),
    "rb1": ((1, 1, 0), (1, 1, 1)),
    "r3": ((0, 3, 0), (0, 3, 1)),
    "r4": ((0, 4, 0),),
    "rb2": ((1, 2, 0), (1, 2, 1)),
    "f3": ((1, 3, 0), (1, 3, 1)),
    "f4": ((1, 4, 0),),
}
BLOCK_FROM = tuple(
    tuple((dx, steps, c, 0) for dx, steps, c in PARTS_OF[name])
    for name in ("k2", "b2", "r1", "r2", "rb1", "r3", "r4", "rb2", "f3", "f4")
) + tuple(
    tuple((dx, steps, 1 - c, 1) for name in names for dx, steps, c in PARTS_OF[name])
    for names in (("r1", "r2"), ("rb1", "r3", "r4"), ("rb2", "f3", "f4"))
)


def seq_at(x0, z, core, part):
    dx, steps, other, far_ring = part
    turn = jnp.where((core + far_ring) % 2 == 0, ZS - steps, steps)
    return ((x0 + dx) % 2 * ZS + (z + turn) % ZS) * 2 + (core + other) % 2


def add_up(first, *rest):
    total = first.astype(jnp.float32)
    for r in rest:
        total = total + r.astype(jnp.float32)
    return total


def scatter_sums(part, residual):
    p = dict(zip(FEATURE_FROM, part))
    n = residual.shape[0] // 2
    bf = jnp.bfloat16
    far = x_flip(p[(2, 1)])
    from_low = y_up(p[(1, 1)])
    from_high = y_down(p[(-1, 1)])
    c = add_up(p[(2, 0)], far).astype(bf)
    c_low = y_up(c[:n])
    c_high = y_down(c[n:])
    rx = x_flip(add_up(p[(0, 1)], from_low, from_high).astype(bf))
    up = p[(1, 0)]
    down = p[(-1, 0)]
    up = jnp.concatenate([add_up(up[:n], c_low).astype(bf), up[n:]], axis=0)
    down = jnp.concatenate([down[:n], add_up(down[n:], c_high).astype(bf)], axis=0)
    ru = y_up(up)
    rd = y_down(down)
    return add_up(residual, p[(0, 0)], rx, ru, rd).astype(bf)


def dot_f32(a, b):
    return jnp.dot(a, b, preferred_element_type=jnp.float32)


def seq_place():
    return tuple(lax.axis_index(a) for a in SEQ)


def first_block_here():
    x0, z, core = seq_place()
    return ((x0 * ZS + z) * 2 + core) * QB


def head_at(part):
    y, xh = lax.axis_index("head_0"), lax.axis_index("head_1")
    dy, dx = part
    return (y + (dy + YS) % YS) % YS * XS + (xh + dx) % XS


def joined(quarter, whole):
    for k in range(2):
        for half in range(2):
            whole[k, half * HALF : (half + 1) * HALF, :] = quarter[2 * k + half][...]


def project(gain_ref, full, whole, rows, weights):
    squares = jnp.zeros((HALF, 128), jnp.float32)
    sums = [jnp.zeros((HALF, w.shape[1]), jnp.float32) for w in weights]
    for k, part in enumerate(FEATURE_FROM):
        piece = full[k][rows, :] if k < 6 else whole[k - 6, rows, :]
        h = head_at(part)
        x = piece.astype(jnp.float32)
        x2 = x * x
        for c in range(4):
            squares = squares + x2[:, c * 128 : (c + 1) * 128]
        scaled = (x * gain_ref[pl.ds(h, 1), :]).astype(jnp.bfloat16)
        span = pl.ds(pl.multiple_of(h * 512, 512), 512)
        for j, w in enumerate(weights):
            sums[j] = sums[j] + dot_f32(scaled, w[span, :])
    total = jnp.sum(squares, axis=1, keepdims=True)
    return sums, lax.rsqrt(total * (1.0 / MODEL_WIDTH) + EPSILON)


def rope(u, cos, sin):
    return u * cos + pltpu.roll(u, 64, 1) * sin


def kv_kernel(gain_ref, cos_ref, sin_ref, *refs):
    full, quarter, (wk_ref, wv_ref, out_ref, whole) = refs[:6], refs[6:10], refs[10:]
    joined(quarter, whole)

    def body(half, _):
        rows = pl.ds(pl.multiple_of(half * HALF, HALF), HALF)
        (k, v), scale = project(gain_ref, full, whole, rows, (wk_ref, wv_ref))
        out_ref[rows, :128] = rope(k * scale, cos_ref[rows, :], sin_ref[rows, :]).astype(jnp.bfloat16)
        out_ref[rows, 128:] = (v * scale).astype(jnp.bfloat16)
        return 0

    lax.fori_loop(0, 2, body, 0)


def q_kernel(gain_ref, dil_ref, width_ref, cos_ref, sin_ref, *refs):
    full, quarter, (wq_ref, out_ref, list_ref, whole) = refs[:6], refs[6:10], refs[10:]
    joined(quarter, whole)
    first = first_block_here()
    for j in range(QB):
        i = first + j
        low = i - width_ref[j] + 1
        start = jnp.maximum(low, 0)
        count = jnp.int32(0)
        for e in range(DILATION_COUNT):
            b = dil_ref[i, e]
            list_ref[j, 1 + count] = b
            count = count + jnp.where(b < low, 1, 0)

        def near(t, _):
            list_ref[j, 1 + count + t] = start + t
            return 0

        lax.fori_loop(0, i - start, near, 0)
        list_ref[j, 0] = count + i - start

    def body(half, _):
        rows = pl.ds(pl.multiple_of(half * HALF, HALF), HALF)
        (q,), scale = project(gain_ref, full, whole, rows, (wq_ref,))
        scale = scale * SCORE_FACTOR
        for g in range(4):
            cols = slice(g * 128, (g + 1) * 128)
            out_ref[rows, cols] = rope(
                q[:, cols] * scale, cos_ref[rows, :], sin_ref[rows, :]
            ).astype(jnp.bfloat16)
        return 0

    lax.fori_loop(0, 2, body, 0)


def out_kernel(which, at_ref, w_ref, *out_refs):
    for k, o in zip(which, out_refs):
        cols = pl.ds(pl.multiple_of(head_at(FEATURE_FROM[k]) * 512, 512), 512)
        o[...] = dot_f32(at_ref[...], w_ref[:, cols]).astype(jnp.bfloat16)


def attention_kernel(list_ref, q_ref, *refs):
    kv_in, (out_ref, buf, acc, top, sems) = refs[: len(BLOCK_FROM)], refs[len(BLOCK_FROM) :]
    x0, z, core = seq_place()
    first_block = first_block_here()
    copies = []
    for ref, parts in zip(kv_in, BLOCK_FROM):
        for s, part in enumerate(parts):
            dest = pl.multiple_of(seq_at(x0, z, core, part) * ROWS, ROWS)
            c = pltpu.make_async_copy(
                ref.at[pl.ds(s * ROWS, ROWS), :], buf.at[pl.ds(dest, ROWS), :], sems.at[len(copies)]
            )
            c.start()
            copies.append(c)
    for c in copies:
        c.wait()
    ones = jnp.ones((GROUP * BLOCK, 128), jnp.bfloat16)

    def load(blocks):
        keys, values = [], []
        for b in blocks:
            r = pl.ds(pl.multiple_of(b * BLOCK, BLOCK), BLOCK)
            keys.append(buf[r, :128])
            values.append(buf[r, 128:])
        values = jnp.concatenate(values, axis=0)
        return jnp.concatenate(keys, axis=0), jnp.concatenate([values, ones], axis=1)

    def one_block(j, _):
        i = first_block + j
        total = list_ref[j, 0]
        rest = lax.rem(total, GROUP)
        rows = pl.ds(pl.multiple_of(j * BLOCK, BLOCK), BLOCK)

        def queries(half):
            return jnp.concatenate(
                [q_ref[rows, c * 128 : (c + 1) * 128] for c in (2 * half, 2 * half + 1)], axis=0
            )

        keys, values = load(
            [i] + [jnp.where(t < rest, list_ref[j, 1 + t], i) for t in range(GROUP - 1)]
        )
        shape = (2 * BLOCK, GROUP * BLOCK)
        col = lax.broadcasted_iota(jnp.int32, shape, 1)
        row = lax.broadcasted_iota(jnp.int32, shape, 0) & (BLOCK - 1)
        limit = jnp.where(col < BLOCK, row + 1, (1 + rest) * BLOCK)
        for half in range(2):
            s = lax.dot_general(
                queries(half), keys, (((1,), (1,)), ((), ())), preferred_element_type=jnp.float32
            )
            s = jnp.where(col < limit, s, NEGATIVE)
            m = jnp.max(s, axis=1, keepdims=True)
            p = jnp.exp2(s - m).astype(jnp.bfloat16)
            acc[half] = dot_f32(p, values)
            top[half] = jnp.broadcast_to(m, (2 * BLOCK, 128))

        def step(g, _):
            t = 1 + rest + g * GROUP
            keys, values = load([list_ref[j, t + e] for e in range(GROUP)])
            for half in range(2):
                s = lax.dot_general(
                    queries(half), keys, (((1,), (1,)), ((), ())), preferred_element_type=jnp.float32
                )
                old = top[half]
                new = jnp.maximum(old, jnp.max(s, axis=1, keepdims=True))
                fade = jnp.exp2(old - new)
                p = jnp.exp2(s - jnp.concatenate([new] * GROUP, axis=1)).astype(jnp.bfloat16)
                acc[half] = acc[half] * jnp.concatenate([fade] * 2, axis=1) + dot_f32(p, values)
                top[half] = new
            return 0

        lax.fori_loop(0, lax.div(total, GROUP), step, 0)
        for half in range(2):
            a = acc[half]
            o = (a[:, :128] / a[:, 128:]).astype(jnp.bfloat16)
            out_ref[rows, (2 * half) * 128 : (2 * half + 1) * 128] = o[:BLOCK]
            out_ref[rows, (2 * half + 1) * 128 : (2 * half + 2) * 128] = o[BLOCK:]
        return 0

    lax.fori_loop(0, QB, one_block, 0)


VMEM = pl.BlockSpec(memory_space=pltpu.VMEM)
SMEM = pl.BlockSpec(memory_space=pltpu.SMEM)
ANY = pl.BlockSpec(memory_space=pl.ANY)
bf16 = jnp.bfloat16


def local_attention(lists, q, gathered):
    return pl.pallas_call(
        attention_kernel,
        out_shape=jax.ShapeDtypeStruct((ROWS, 512), bf16),
        in_specs=[SMEM, VMEM] + [ANY] * len(gathered),
        out_specs=VMEM,
        scratch_shapes=[
            pltpu.VMEM((32 * ROWS, 256), bf16),
            pltpu.VMEM((2, 2 * BLOCK, 256), jnp.float32),
            pltpu.VMEM((2, 2 * BLOCK, 128), jnp.float32),
            pltpu.SemaphoreType.DMA((32,)),
        ],
        cost_estimate=pl.CostEstimate(flops=2 * 10**10, transcendentals=10**7, bytes_accessed=10**7),
        name="attend",
    )(lists, q, *gathered)


def shards(tokens, norm_gain, w_query, w_key, w_value, w_output, widths, dilation):
    half_size = HEAD_WIDTH // 2
    positions = first_block_here() * BLOCK + jnp.arange(ROWS, dtype=jnp.int32)
    frequency = ROPE_BASE ** (-jnp.arange(half_size, dtype=jnp.float32) * 2.0 / HEAD_WIDTH)
    angles = positions.astype(jnp.float32)[:, None] * frequency[None, :]
    cosine, sine = jnp.cos(angles), jnp.sin(angles)
    cosine = jnp.concatenate([cosine, cosine], axis=1)
    sine = jnp.concatenate([-sine, sine], axis=1)
    gain = norm_gain.reshape(8, 512)

    full, quarter = gather_features(tokens)
    pieces = full + quarter
    kv = pl.pallas_call(
        kv_kernel,
        out_shape=jax.ShapeDtypeStruct((ROWS, 256), bf16),
        in_specs=[VMEM] * 15,
        out_specs=VMEM,
        scratch_shapes=[pltpu.VMEM((2, ROWS, 512), bf16)],
        cost_estimate=pl.CostEstimate(flops=10**9, transcendentals=0, bytes_accessed=6 * 10**6),
        name="keys_values",
    )(gain, cosine, sine, *pieces, w_key, w_value)
    gathered = gather_blocks(kv)
    query_call = pl.pallas_call(
        q_kernel,
        out_shape=[
            jax.ShapeDtypeStruct((ROWS, 512), bf16),
            jax.ShapeDtypeStruct((QB, 64), jnp.int32),
        ],
        in_specs=[VMEM] + [SMEM] * 2 + [VMEM] * 13,
        out_specs=[VMEM, SMEM],
        scratch_shapes=[pltpu.VMEM((2, ROWS, 512), bf16)],
        cost_estimate=pl.CostEstimate(flops=4 * 10**9, transcendentals=0, bytes_accessed=10**7),
        name="queries",
    )
    q, lists = query_call(gain, dilation, widths, cosine, sine, *pieces, w_query)
    attention = local_attention(lists, q, gathered)

    def shares(which):
        return pl.pallas_call(
            functools.partial(out_kernel, which),
            out_shape=[jax.ShapeDtypeStruct((ROWS, 512), bf16)] * len(which),
            in_specs=[VMEM, VMEM],
            out_specs=[VMEM] * len(which),
            cost_estimate=pl.CostEstimate(
                flops=len(which) * 2**28, transcendentals=0, bytes_accessed=len(which) * 2**20
            ),
            name="project_out",
        )(attention, w_output)

    first = (7, 4, 5)
    second = (6, 1, 2, 3, 0)
    part = dict(zip(first, shares(first)))
    part.update(zip(second, shares(second)))
    return scatter_sums([part[k] for k in range(8)], tokens)


def solution(mesh):
    split = Mesh(mesh.devices.reshape(2, ZS, 2, YS, XS), SEQ + HEAD)
    placed = (
        P(SEQ, HEAD),
        P(),
        P(None, HEAD),
        P(None, HEAD),
        P(None, HEAD),
        P(HEAD, None),
        P(SEQ),
        P(),
    )
    return jax.shard_map(
        shards, mesh=split, in_specs=placed, out_specs=P(SEQ, HEAD), check_vma=False
    )
```

profile of v0, /device:TPU:6, one launch (start us, length us, event | category | flops | bytes accessed | tf_op | source)
XLA Modules:
  0.0 190.1 jit_solution(2361575039327154543)
XLA Ops:
  0.0 3.0 %collective-permute-start.2 = (bf16[512,512]{1,0:T(8,128)(2,1)}, bf16[512,512]{1,0:T(8,128)(2,1)S(1)}, u32[]{:S(2)}, u32[]{:S(2)}) collective-permute-start(bf16[512,512]{1,0:T(8,128)(2,1)} %refs_0_.3), channel_id=1, source_target_pairs={{0,6},{2,0},{4,2},{6,4},{1,7},{3,1},{5,3},{7,5},{8,14},{10,8},{12,... | collective-permute-start | bytes 1572872 | tf_op jit(solution)/shard_map/ppermute | solution.py:30
  4.4 10.1 %collective-permute-done.2.refs_3_ = bf16[512,512]{1,0:T(8,128)(2,1)S(1)} collective-permute-done((bf16[512,512]{1,0:T(8,128)(2,1)}, bf16[512,512]{1,0:T(8,128)(2,1)S(1)}, u32[]{:S(2)}, u32[]{:S(2)}) %collective-permute-start.2) | collective-permute-done | bytes 524320 | tf_op jit(solution)/shard_map/ppermute | solution.py:30
  14.5 3.7 %collective-permute-start.6 = (bf16[256,512]{1,0:T(8,128)(2,1)S(1)}, bf16[256,512]{1,0:T(8,128)(2,1)S(1)}, u32[]{:S(2)}, u32[]{:S(2)}) collective-permute-start(bf16[256,512]{1,0:T(8,128)(2,1)S(1)} %slice.37), channel_id=1, source_target_pairs={{0,6},{2,0},{4,2},{6,4},{1,7},{3,1},{5,3},{7,5},{8,14},{10,8},{12,... | collective-permute-start | bytes 786440 | tf_op jit(solution)/shard_map/ppermute | solution.py:30
  19.0 3.2 %collective-permute-start.4 = (bf16[512,512]{1,0:T(8,128)(2,1)S(1)}, bf16[512,512]{1,0:T(8,128)(2,1)S(1)}, u32[]{:S(2)}, u32[]{:S(2)}) collective-permute-start(bf16[512,512]{1,0:T(8,128)(2,1)S(1)} %collective-permute-done.refs_1_), channel_id=1, source_target_pairs={{0,6},{2,0},{4,2},{6,4},{1,7},{3,1},{5,3},{7,5},{8,14},{10,8},{12,... | collective-permute-start | bytes 1572872 | tf_op jit(solution)/shard_map/ppermute | solution.py:30
  26.3 3.3 %collective-permute-done.5.refs_6_ = bf16[256,512]{1,0:T(8,128)(2,1)S(1)} collective-permute-done((bf16[256,512]{1,0:T(8,128)(2,1)}, bf16[256,512]{1,0:T(8,128)(2,1)S(1)}, u32[]{:S(2)}, u32[]{:S(2)}) %collective-permute-start.5) | collective-permute-done | bytes 262176 | tf_op jit(solution)/shard_map/ppermute | solution.py:30
  39.3 6.4 %keys_values.1 = bf16[512,256]{1,0:T(8,128)(2,1)} custom-call(f32[8,512]{1,0:T(8,128)} %reshape.14.gain_ref, f32[512,128]{1,0:T(8,128)} %get-tuple-element.30.cos_ref, f32[512,128]{1,0:T(8,128)} %get-tuple-element.31.sin_ref, bf16[512,512]{1,0:T(8,128)(2,1)} %refs_0_.3, bf16[512,512]{1,0:T(8,128)(2,1)} %copy-done.4, bf16[512,512]{1,0:T(8,128)(2,1)} %copy-done.2, ...), custom_call_target="tpu_custom_call" | custom-call | flops 1000000000 | bytes 6000000 | tf_op jit(solution)/shard_map/keys_values/pallas_call | solution.py:372
  50.5 11.1 %collective-permute-done.12.refs_2_ = bf16[1024,256]{1,0:T(8,128)(2,1)S(1)} collective-permute-done((bf16[1024,256]{1,0:T(8,128)(2,1)S(1)}, bf16[1024,256]{1,0:T(8,128)(2,1)S(1)}, u32[]{:S(2)}, u32[]{:S(2)}) %collective-permute-start.12) | collective-permute-done | bytes 524320 | tf_op jit(solution)/shard_map/ppermute | solution.py:75
  62.4 7.6 %collective-permute-done.10 = bf16[512,256]{1,0:T(8,128)(2,1)S(1)} collective-permute-done((bf16[512,256]{1,0:T(8,128)(2,1)}, bf16[512,256]{1,0:T(8,128)(2,1)S(1)}, u32[]{:S(2)}, u32[]{:S(2)}) %collective-permute-start.10) | collective-permute-done | bytes 262176 | tf_op jit(solution)/shard_map/ppermute | solution.py:30
  72.4 10.0 %collective-permute-done.15.refs_5_ = bf16[1024,256]{1,0:T(8,128)(2,1)S(1)} collective-permute-done((bf16[1024,256]{1,0:T(8,128)(2,1)S(1)}, bf16[1024,256]{1,0:T(8,128)(2,1)S(1)}, u32[]{:S(2)}, u32[]{:S(2)}) %collective-permute-start.15) | collective-permute-done | bytes 524320 | tf_op jit(solution)/shard_map/ppermute | solution.py:75
  82.5 5.5 %collective-permute-done.14.refs_4_ = bf16[1024,256]{1,0:T(8,128)(2,1)S(1)} collective-permute-done((bf16[1024,256]{1,0:T(8,128)(2,1)S(1)}, bf16[1024,256]{1,0:T(8,128)(2,1)S(1)}, u32[]{:S(2)}, u32[]{:S(2)}) %collective-permute-start.14) | collective-permute-done | bytes 524320 | tf_op jit(solution)/shard_map/ppermute | solution.py:75
  91.8 6.6 %collective-permute-done.17.refs_7_ = bf16[1024,256]{1,0:T(8,128)(2,1)S(1)} collective-permute-done((bf16[1024,256]{1,0:T(8,128)(2,1)S(1)}, bf16[1024,256]{1,0:T(8,128)(2,1)S(1)}, u32[]{:S(2)}, u32[]{:S(2)}) %collective-permute-start.17) | collective-permute-done | bytes 524320 | tf_op jit(solution)/shard_map/ppermute | solution.py:75
  98.4 8.7 %collective-permute-done.19.refs_9_ = bf16[512,256]{1,0:T(8,128)(2,1)S(1)} collective-permute-done((bf16[512,256]{1,0:T(8,128)(2,1)S(1)}, bf16[512,256]{1,0:T(8,128)(2,1)S(1)}, u32[]{:S(2)}, u32[]{:S(2)}) %collective-permute-start.19) | collective-permute-done | bytes 262176 | tf_op jit(solution)/shard_map/ppermute | solution.py:30
  109.7 7.9 %queries.1 = (bf16[512,512]{1,0:T(8,128)(2,1)}, s32[4,64]{1,0:T(4,128)}) custom-call(f32[8,512]{1,0:T(8,128)} %reshape.14.gain_ref, s32[128,8]{1,0:T(8,128)} %copy.9.dil_ref, s32[4]{0:T(128)} %width_ref.1, f32[512,128]{1,0:T(8,128)} %get-tuple-element.30.cos_ref, f32[512,128]{1,0:T(8,128)} %get-tuple-element.31.sin_ref, bf16[512,512]{1,0:T(8,128)(2,1)} %refs_0_.3, ...), custom_call_target="tpu_custom_call" | custom-call | flops 4000000000 | bytes 10000000 | tf_op jit(solution)/shard_map/queries/pallas_call | solution.py:394
  117.7 25.5 %attend.1.at_ref = bf16[512,512]{1,0:T(8,128)(2,1)} custom-call(s32[4,64]{1,0:T(4,128)} %get-tuple-element.15.list_ref, bf16[512,512]{1,0:T(8,128)(2,1)} %get-tuple-element.16.q_ref, bf16[1024,256]{1,0:T(8,128)(2,1)} %copy-done.12, bf16[1024,256]{1,0:T(8,128)(2,1)} %copy-done.23, bf16[1024,256]{1,0:T(8,128)(2,1)} %copy-done.13, ...), custom_call_target="tpu_custom_call" | custom-call | flops 20000000000 | bytes 10000000 | tf_op jit(solution)/shard_map/attend/pallas_call | solution.py:344
  143.1 4.2 %project_out.3 = (bf16[512,512]{1,0:T(8,128)(2,1)}, bf16[512,512]{1,0:T(8,128)(2,1)}, bf16[512,512]{1,0:T(8,128)(2,1)}) custom-call(bf16[512,512]{1,0:T(8,128)(2,1)} %attend.1.at_ref, bf16[512,4096]{1,0:T(8,128)(2,1)} %w_ref.3), custom_call_target="tpu_custom_call" | custom-call | flops 805306368 | bytes 3145728 | tf_op jit(solution)/shard_map/project_out/pallas_call | solution.py:398
  148.7 3.2 %collective-permute-start.24 = (bf16[512,512]{1,0:T(8,128)(2,1)}, bf16[512,512]{1,0:T(8,128)(2,1)S(1)}, u32[]{:S(2)}, u32[]{:S(2)}) collective-permute-start(bf16[512,512]{1,0:T(8,128)(2,1)} %get-tuple-element.20), channel_id=1, source_target_pairs={{0,6},{2,0},{4,2},{6,4},{1,7},{3,1},{5,3},{7,5},{8,14},{10,8},{12,... | collective-permute-start | bytes 1572872 | tf_op jit(solution)/shard_map/ppermute | solution.py:30
  151.9 4.7 %project_out.2 = (bf16[512,512]{1,0:T(8,128)(2,1)}, bf16[512,512]{1,0:T(8,128)(2,1)}, bf16[512,512]{1,0:T(8,128)(2,1)}, bf16[512,512]{1,0:T(8,128)(2,1)}, bf16[512,512]{1,0:T(8,128)(2,1)}) custom-call(bf16[512,512]{1,0:T(8,128)(2,1)} %attend.1.at_ref, bf16[512,4096]{1,0:T(8,128)(2,1)} %w_ref.3), custom_call_target="tpu_custom_call" | custom-call | flops 1342177280 | bytes 5242880 | tf_op jit(solution)/shard_map/project_out/pallas_call | solution.py:398
  158.6 4.3 %collective-permute-done.26 = bf16[512,512]{1,0:T(8,128)(2,1)S(1)} collective-permute-done((bf16[512,512]{1,0:T(8,128)(2,1)}, bf16[512,512]{1,0:T(8,128)(2,1)S(1)}, u32[]{:S(2)}, u32[]{:S(2)}) %collective-permute-start.26) | collective-permute-done | bytes 524320 | tf_op jit(solution)/shard_map/ppermute | solution.py:30
  164.2 3.2 %collective-permute-start.29 = (bf16[256,512]{1,0:T(8,128)(2,1)S(1)}, bf16[256,512]{1,0:T(8,128)(2,1)S(1)}, u32[]{:S(2)}, u32[]{:S(2)}) collective-permute-start(bf16[256,512]{1,0:T(8,128)(2,1)S(1)} %get-tuple-element.26), channel_id=1, source_target_pairs={{0,6},{2,0},{4,2},{6,4},{1,7},{3,1},{5,3},{7,5},{8,14},{10,8},{12,... | collective-permute-start | bytes 786440 | tf_op jit(solution)/shard_map/ppermute | solution.py:30
  169.2 2.9 %collective-permute-done.29 = bf16[256,512]{1,0:T(8,128)(2,1)S(1)} collective-permute-done((bf16[256,512]{1,0:T(8,128)(2,1)S(1)}, bf16[256,512]{1,0:T(8,128)(2,1)S(1)}, u32[]{:S(2)}, u32[]{:S(2)}) %collective-permute-start.29) | collective-permute-done | bytes 262176 | tf_op jit(solution)/shard_map/ppermute | solution.py:30
  172.2 3.8 %collective-permute-start.30 = (bf16[512,512]{1,0:T(8,128)(2,1)S(1)}, bf16[512,512]{1,0:T(8,128)(2,1)S(1)}, u32[]{:S(2)}, u32[]{:S(2)}) collective-permute-start(bf16[512,512]{1,0:T(8,128)(2,1)S(1)} %pad_maximum_fusion.5), channel_id=1, source_target_pairs={{0,6},{2,0},{4,2},{6,4},{1,7},{3,1},{5,3},{7,5},{8,14},{10,8},{12,... | collective-permute-start | bytes 1572872 | tf_op jit(solution)/shard_map/ppermute | solution.py:30
  176.2 5.6 %collective-permute-done.25 = bf16[512,512]{1,0:T(8,128)(2,1)S(1)} collective-permute-done((bf16[512,512]{1,0:T(8,128)(2,1)S(1)}, bf16[512,512]{1,0:T(8,128)(2,1)S(1)}, u32[]{:S(2)}, u32[]{:S(2)}) %collective-permute-start.25) | collective-permute-done | bytes 524320 | tf_op jit(solution)/shard_map/ppermute | solution.py:30
  181.8 3.6 %collective-permute-done.30 = bf16[512,512]{1,0:T(8,128)(2,1)S(1)} collective-permute-done((bf16[512,512]{1,0:T(8,128)(2,1)S(1)}, bf16[512,512]{1,0:T(8,128)(2,1)S(1)}, u32[]{:S(2)}, u32[]{:S(2)}) %collective-permute-start.30) | collective-permute-done | bytes 524320 | tf_op jit(solution)/shard_map/ppermute | solution.py:30
  185.4 3.6 %collective-permute-done.28 = bf16[512,512]{1,0:T(8,128)(2,1)S(1)} collective-permute-done((bf16[512,512]{1,0:T(8,128)(2,1)S(1)}, bf16[512,512]{1,0:T(8,128)(2,1)S(1)}, u32[]{:S(2)}, u32[]{:S(2)}) %collective-permute-start.28) | collective-permute-done | bytes 524320 | tf_op jit(solution)/shard_map/ppermute | solution.py:30
  (118 shorter events, 38.3 us)
Async XLA Ops:
  0.0 14.5 %collective-permute-start.2 = (bf16[512,512]{1,0:T(8,128)(2,1)}, bf16[512,512]{1,0:T(8,128)(2,1)S(1)}, u32[]{:S(2)}, u32[]{:S(2)}) collective-permute-start(bf16[512,512]{1,0:T(8,128)(2,1)} %refs_0_.3), channel_id=1, source_target_pairs={{0,6},{2,0},{4,2},{6,4},{1,7},{3,1},{5,3},{7,5},{8,14},{10,8},{12,... | collective-permute-start | bytes 1572872 | tf_op jit(solution)/shard_map/ppermute | solution.py:30
  3.0 15.2 %collective-permute-start.1 = (bf16[512,512]{1,0:T(8,128)(2,1)}, bf16[512,512]{1,0:T(8,128)(2,1)S(1)}, u32[]{:S(2)}, u32[]{:S(2)}) collective-permute-start(bf16[512,512]{1,0:T(8,128)(2,1)} %refs_0_.3), channel_id=1, source_target_pairs={{0,2},{2,4},{4,6},{6,0},{1,3},{3,5},{5,7},{7,1},{8,10},{10,12},{12... | collective-permute-start | bytes 1572872 | tf_op jit(solution)/shard_map/ppermute | solution.py:30
  3.0 16.0 %collective-permute-start = (bf16[512,512]{1,0:T(8,128)(2,1)}, bf16[512,512]{1,0:T(8,128)(2,1)S(1)}, u32[]{:S(2)}, u32[]{:S(2)}) collective-permute-start(bf16[512,512]{1,0:T(8,128)(2,1)} %refs_0_.3), channel_id=1, source_target_pairs={{0,1},{1,0},{2,3},{3,2},{4,5},{5,4},{6,7},{7,6},{8,9},{9,8},{10,11... | collective-permute-start | bytes 1572872 | tf_op jit(solution)/shard_map/ppermute | solution.py:30
  14.5 10.4 %collective-permute-start.6 = (bf16[256,512]{1,0:T(8,128)(2,1)S(1)}, bf16[256,512]{1,0:T(8,128)(2,1)S(1)}, u32[]{:S(2)}, u32[]{:S(2)}) collective-permute-start(bf16[256,512]{1,0:T(8,128)(2,1)S(1)} %slice.37), channel_id=1, source_target_pairs={{0,6},{2,0},{4,2},{6,4},{1,7},{3,1},{5,3},{7,5},{8,14},{10,8},{12,... | collective-permute-start | bytes 786440 | tf_op jit(solution)/shard_map/ppermute | solution.py:30
  19.0 10.6 %collective-permute-start.5 = (bf16[256,512]{1,0:T(8,128)(2,1)}, bf16[256,512]{1,0:T(8,128)(2,1)S(1)}, u32[]{:S(2)}, u32[]{:S(2)}) collective-permute-start(bf16[256,512]{1,0:T(8,128)(2,1)} %slice.36), channel_id=1, source_target_pairs={{0,2},{2,4},{4,6},{6,0},{1,3},{3,5},{5,7},{7,1},{8,10},{10,12},{12... | collective-permute-start | bytes 786440 | tf_op jit(solution)/shard_map/ppermute | solution.py:30
  19.0 18.7 %collective-permute-start.4 = (bf16[512,512]{1,0:T(8,128)(2,1)S(1)}, bf16[512,512]{1,0:T(8,128)(2,1)S(1)}, u32[]{:S(2)}, u32[]{:S(2)}) collective-permute-start(bf16[512,512]{1,0:T(8,128)(2,1)S(1)} %collective-permute-done.refs_1_), channel_id=1, source_target_pairs={{0,6},{2,0},{4,2},{6,4},{1,7},{3,1},{5,3},{7,5},{8,14},{10,8},{12,... | collective-permute-start | bytes 1572872 | tf_op jit(solution)/shard_map/ppermute | solution.py:30
  22.2 16.3 %collective-permute-start.3 = (bf16[512,512]{1,0:T(8,128)(2,1)S(1)}, bf16[512,512]{1,0:T(8,128)(2,1)S(1)}, u32[]{:S(2)}, u32[]{:S(2)}) collective-permute-start(bf16[512,512]{1,0:T(8,128)(2,1)S(1)} %collective-permute-done.refs_1_), channel_id=1, source_target_pairs={{0,2},{2,4},{4,6},{6,0},{1,3},{3,5},{5,7},{7,1},{8,10},{10,12},{12... | collective-permute-start | bytes 1572872 | tf_op jit(solution)/shard_map/ppermute | solution.py:30
  24.9 10.0 %collective-permute-start.8 = (bf16[256,512]{1,0:T(8,128)(2,1)S(1)}, bf16[256,512]{1,0:T(8,128)(2,1)S(1)}, u32[]{:S(2)}, u32[]{:S(2)}) collective-permute-start(bf16[256,512]{1,0:T(8,128)(2,1)S(1)} %collective-permute-done.6.refs_7_), channel_id=1, source_target_pairs={{0,1},{1,0},{2,3},{3,2},{4,5},{5,4},{6,7},{7,6},{8,9},{9,8},{10,11... | collective-permute-start | bytes 786440 | tf_op jit(solution)/shard_map/ppermute | solution.py:30
  48.5 13.1 %collective-permute-start.12 = (bf16[1024,256]{1,0:T(8,128)(2,1)S(1)}, bf16[1024,256]{1,0:T(8,128)(2,1)S(1)}, u32[]{:S(2)}, u32[]{:S(2)}) collective-permute-start(bf16[1024,256]{1,0:T(8,128)(2,1)S(1)} %pad_maximum_fusion.3.refs_0_), channel_id=1, source_target_pairs={{0,16},{8,120},{16,32},{24,8},{32,48},{40,24},{48,64},{56,40},{64,... | collective-permute-start | bytes 1572872 | tf_op jit(solution)/shard_map/ppermute | solution.py:75
  61.6 10.4 %collective-permute-start.13 = (bf16[1024,256]{1,0:T(8,128)(2,1)S(1)}, bf16[1024,256]{1,0:T(8,128)(2,1)S(1)}, u32[]{:S(2)}, u32[]{:S(2)}) collective-permute-start(bf16[1024,256]{1,0:T(8,128)(2,1)S(1)} %collective-permute-done.12.refs_2_), channel_id=1, source_target_pairs={{0,16},{8,120},{16,32},{24,8},{32,48},{40,24},{48,64},{56,40},{64,... | collective-permute-start | bytes 1572872 | tf_op jit(solution)/shard_map/ppermute | solution.py:75
  72.0 10.4 %collective-permute-start.15 = (bf16[1024,256]{1,0:T(8,128)(2,1)S(1)}, bf16[1024,256]{1,0:T(8,128)(2,1)S(1)}, u32[]{:S(2)}, u32[]{:S(2)}) collective-permute-start(bf16[1024,256]{1,0:T(8,128)(2,1)S(1)} %collective-permute-done.13.refs_3_), channel_id=1, source_target_pairs={{0,16},{8,120},{16,32},{24,8},{32,48},{40,24},{48,64},{56,40},{64,... | collective-permute-start | bytes 1572872 | tf_op jit(solution)/shard_map/ppermute | solution.py:75
  72.3 15.7 %collective-permute-start.14 = (bf16[1024,256]{1,0:T(8,128)(2,1)S(1)}, bf16[1024,256]{1,0:T(8,128)(2,1)S(1)}, u32[]{:S(2)}, u32[]{:S(2)}) collective-permute-start(bf16[1024,256]{1,0:T(8,128)(2,1)S(1)} %constant_dynamic-update-slice_fusion.refs_1_), channel_id=1, source_target_pairs={{0,16},{8,120},{16,32},{24,8},{32,48},{40,24},{48,64},{56,40},{64,... | collective-permute-start | bytes 1572872 | tf_op jit(solution)/shard_map/ppermute | solution.py:75
  88.0 10.4 %collective-permute-start.17 = (bf16[1024,256]{1,0:T(8,128)(2,1)S(1)}, bf16[1024,256]{1,0:T(8,128)(2,1)S(1)}, u32[]{:S(2)}, u32[]{:S(2)}) collective-permute-start(bf16[1024,256]{1,0:T(8,128)(2,1)S(1)} %collective-permute-done.14.refs_4_), channel_id=1, source_target_pairs={{0,16},{8,120},{16,32},{24,8},{32,48},{40,24},{48,64},{56,40},{64,... | collective-permute-start | bytes 1572872 | tf_op jit(solution)/shard_map/ppermute | solution.py:75
  88.0 19.1 %collective-permute-start.18 = (bf16[1024,256]{1,0:T(8,128)(2,1)S(1)}, bf16[1024,256]{1,0:T(8,128)(2,1)S(1)}, u32[]{:S(2)}, u32[]{:S(2)}) collective-permute-start(bf16[1024,256]{1,0:T(8,128)(2,1)S(1)} %collective-permute-done.15.refs_5_), channel_id=1, source_target_pairs={{0,128},{128,0},{1,129},{129,1},{2,130},{130,2},{3,131},{131,3},{4... | collective-permute-start | bytes 1572872 | tf_op jit(solution)/shard_map/ppermute | solution.py:30
  90.8 16.3 %collective-permute-start.19 = (bf16[512,256]{1,0:T(8,128)(2,1)S(1)}, bf16[512,256]{1,0:T(8,128)(2,1)S(1)}, u32[]{:S(2)}, u32[]{:S(2)}) collective-permute-start(bf16[512,256]{1,0:T(8,128)(2,1)S(1)} %collective-permute-done.16.refs_6_), channel_id=1, source_target_pairs={{0,128},{128,0},{1,129},{129,1},{2,130},{130,2},{3,131},{131,3},{4... | collective-permute-start | bytes 786440 | tf_op jit(solution)/shard_map/ppermute | solution.py:30
  91.7 25.9 %collective-permute-start.21 = (bf16[2560,256]{1,0:T(8,128)(2,1)S(1)}, bf16[2560,256]{1,0:T(8,128)(2,1)}, u32[]{:S(2)}, u32[]{:S(2)}) collective-permute-start(bf16[2560,256]{1,0:T(8,128)(2,1)S(1)} %pad_maximum_fusion), channel_id=1, source_target_pairs={{0,8},{8,0},{1,9},{9,1},{2,10},{10,2},{3,11},{11,3},{4,12},{12,4},... | collective-permute-start | bytes 3932168 | tf_op jit(solution)/shard_map/ppermute | solution.py:30
  107.2 10.4 %collective-permute-start.22 = (bf16[2560,256]{1,0:T(8,128)(2,1)S(1)}, bf16[2560,256]{1,0:T(8,128)(2,1)}, u32[]{:S(2)}, u32[]{:S(2)}) collective-permute-start(bf16[2560,256]{1,0:T(8,128)(2,1)S(1)} %pad_maximum_fusion.1), channel_id=1, source_target_pairs={{0,8},{8,0},{1,9},{9,1},{2,10},{10,2},{3,11},{11,3},{4,12},{12,4},... | collective-permute-start | bytes 3932168 | tf_op jit(solution)/shard_map/ppermute | solution.py:30
  147.3 15.6 %collective-permute-start.26 = (bf16[512,512]{1,0:T(8,128)(2,1)}, bf16[512,512]{1,0:T(8,128)(2,1)S(1)}, u32[]{:S(2)}, u32[]{:S(2)}) collective-permute-start(bf16[512,512]{1,0:T(8,128)(2,1)} %get-tuple-element.23), channel_id=1, source_target_pairs={{0,1},{1,0},{2,3},{3,2},{4,5},{5,4},{6,7},{7,6},{8,9},{9,8},{10,11... | collective-permute-start | bytes 1572872 | tf_op jit(solution)/shard_map/ppermute | solution.py:30
  148.7 18.8 %collective-permute-start.23 = (bf16[512,512]{1,0:T(8,128)(2,1)}, bf16[512,512]{1,0:T(8,128)(2,1)S(1)}, u32[]{:S(2)}, u32[]{:S(2)}) collective-permute-start(bf16[512,512]{1,0:T(8,128)(2,1)} %get-tuple-element.19), channel_id=1, source_target_pairs={{0,2},{2,4},{4,6},{6,0},{1,3},{3,5},{5,7},{7,1},{8,10},{10,12},{12... | collective-permute-start | bytes 1572872 | tf_op jit(solution)/shard_map/ppermute | solution.py:30
  148.7 18.8 %collective-permute-start.24 = (bf16[512,512]{1,0:T(8,128)(2,1)}, bf16[512,512]{1,0:T(8,128)(2,1)S(1)}, u32[]{:S(2)}, u32[]{:S(2)}) collective-permute-start(bf16[512,512]{1,0:T(8,128)(2,1)} %get-tuple-element.20), channel_id=1, source_target_pairs={{0,6},{2,0},{4,2},{6,4},{1,7},{3,1},{5,3},{7,5},{8,14},{10,8},{12,... | collective-permute-start | bytes 1572872 | tf_op jit(solution)/shard_map/ppermute | solution.py:30
  164.2 11.8 %collective-permute-start.27 = (bf16[256,512]{1,0:T(8,128)(2,1)S(1)}, bf16[256,512]{1,0:T(8,128)(2,1)S(1)}, u32[]{:S(2)}, u32[]{:S(2)}) collective-permute-start(bf16[256,512]{1,0:T(8,128)(2,1)S(1)} %get-tuple-element.25), channel_id=1, source_target_pairs={{0,2},{2,4},{4,6},{6,0},{1,3},{3,5},{5,7},{7,1},{8,10},{10,12},{12... | collective-permute-start | bytes 786440 | tf_op jit(solution)/shard_map/ppermute | solution.py:30
  167.7 14.0 %collective-permute-start.25 = (bf16[512,512]{1,0:T(8,128)(2,1)S(1)}, bf16[512,512]{1,0:T(8,128)(2,1)S(1)}, u32[]{:S(2)}, u32[]{:S(2)}) collective-permute-start(bf16[512,512]{1,0:T(8,128)(2,1)S(1)} %add_convert_fusion.2), channel_id=1, source_target_pairs={{0,1},{1,0},{2,3},{3,2},{4,5},{5,4},{6,7},{7,6},{8,9},{9,8},{10,11... | collective-permute-start | bytes 1572872 | tf_op jit(solution)/shard_map/ppermute | solution.py:30
  172.2 13.2 %collective-permute-start.30 = (bf16[512,512]{1,0:T(8,128)(2,1)S(1)}, bf16[512,512]{1,0:T(8,128)(2,1)S(1)}, u32[]{:S(2)}, u32[]{:S(2)}) collective-permute-start(bf16[512,512]{1,0:T(8,128)(2,1)S(1)} %pad_maximum_fusion.5), channel_id=1, source_target_pairs={{0,6},{2,0},{4,2},{6,4},{1,7},{3,1},{5,3},{7,5},{8,14},{10,8},{12,... | collective-permute-start | bytes 1572872 | tf_op jit(solution)/shard_map/ppermute | solution.py:30
  176.1 12.9 %collective-permute-start.28 = (bf16[512,512]{1,0:T(8,128)(2,1)S(1)}, bf16[512,512]{1,0:T(8,128)(2,1)S(1)}, u32[]{:S(2)}, u32[]{:S(2)}) collective-permute-start(bf16[512,512]{1,0:T(8,128)(2,1)S(1)} %pad_maximum_fusion.4), channel_id=1, source_target_pairs={{0,2},{2,4},{4,6},{6,0},{1,3},{3,5},{5,7},{7,1},{8,10},{10,12},{12... | collective-permute-start | bytes 1572872 | tf_op jit(solution)/shard_map/ppermute | solution.py:30
  (32 other events, 443.0 us)
where the time goes:
time: 190 us
  waiting for transfers between devices  94.4 us (50%)
  Pallas kernels  48.6 us (26%)
  starting transfers between devices  34 us (18%)
  other arithmetic  7.05 us (4%)
  local copies, waits for them, and re-layouts  5.76 us (3%)
    ppermute x25, waiting for transfers between devices, moved(): return lax.ppermute(x, axis, [(k, (k + step) % size) for k in range(size)])  58.5 us
    ppermute x6, waiting for transfers between devices, ring(): return lax.ppermute(x, ('seq_1', 'seq_2'), pairs)  35.9 us
    ppermute x25, starting transfers between devices, moved(): return lax.ppermute(x, axis, [(k, (k + step) % size) for k in range(size)])  31.8 us
    pallas_call x1, Pallas kernels, local_attention(): pl.pallas_call(attention_kernel, out_shape=jax.ShapeDtypeStruct((ROWS, 51...  25.5 us
    pallas_call x2, Pallas kernels, shares(): pl.pallas_call(functools.partial(out_kernel, which), out_shape=[jax.Shape...  8.83 us
    pallas_call x1, Pallas kernels, shards(): query_call(gain, dilation, widths, cosine, sine, *pieces, w_query)  7.93 us
    pallas_call x1, Pallas kernels, shards(): pl.pallas_call(kv_kernel, out_shape=jax.ShapeDtypeStruct((ROWS, 256), bf1...  6.38 us
  transfers between devices with their start and end apart: 31, of which 21 were waited for; matrix products, arithmetic and copies ran while one was open for 5% of the time, Pallas kernels for 7%

commit v1 on v0

v1 whole, which is shorter than its diff:
```python
import functools
import math

import jax
import jax.numpy as jnp
from jax import lax
from jax.experimental import pallas as pl
from jax.experimental.pallas import tpu as pltpu
from jax.sharding import Mesh
from jax.sharding import PartitionSpec as P

MODEL_WIDTH = 4096
HEAD_WIDTH = 128
BLOCK = 128
DILATION_COUNT = 8
ROWS = 512
HALF = 256
QB = 4
SEQ = ("seq_0", "seq_1", "seq_2")
HEAD = ("head_0", "head_1")
YS, XS, ZS = 4, 2, 8
EPSILON = 1e-05
NEGATIVE = -1e30
ROPE_BASE = 10000.0
SCORE_FACTOR = math.log2(math.e) / math.sqrt(HEAD_WIDTH)
GROUP = 4
LATE = 64


def moved(x, axis, size, step):
    return lax.ppermute(x, axis, [(k, (k + step) % size) for k in range(size)])


def y_up(x):
    return moved(x, "head_0", YS, 1)


def y_down(x):
    return moved(x, "head_0", YS, -1)


def x_flip(x):
    return moved(x, "head_1", XS, 1)


def pair_flip(x):
    return moved(x, "seq_0", 2, 1)


def core_flip(x):
    return moved(x, "seq_2", 2, 1)


def gather_features(a):
    n = a.shape[0] // 2
    b = x_flip(a)
    u = y_up(a)
    d = y_down(a)
    ct = y_up(u[:n])
    cb = y_down(d[n:])
    bu = y_up(b)
    bd = y_down(b)
    et = x_flip(ct)
    eb = x_flip(cb)
    return (a, b, u, d, bu, bd), (ct, cb, et, eb)


FEATURE_FROM = ((0, 0), (0, 1), (-1, 0), (1, 0), (-1, 1), (1, 1), (2, 0), (2, 1))


def ring(x):
    pairs = []
    for z in range(ZS):
        pairs.append((2 * z, 2 * ((z + 1) % ZS)))
        pairs.append((2 * z + 1, 2 * ((z - 1) % ZS) + 1))
    return lax.ppermute(x, ("seq_1", "seq_2"), pairs)


def cat(*v):
    return jnp.concatenate(v, axis=0)


def gather_blocks(k):
    n = k.shape[0]
    k2 = cat(k, core_flip(k))
    b = pair_flip(k)
    r1 = ring(k2)
    b2 = cat(b, core_flip(b))
    r2 = ring(r1)
    rb1 = ring(b2)
    r3 = ring(r2)
    s1 = core_flip(cat(r1, r2))
    rb2 = ring(rb1)
    r4 = ring(r3[:n])
    f3 = pair_flip(r3)
    s2 = core_flip(cat(rb1, r3))
    f4 = pair_flip(r4)
    s3 = core_flip(cat(rb2, r4))
    s4 = core_flip(cat(f3, f4))
    return (k2, b2, r1, r2, rb1, s1), (r3, r4, rb2, f3, f4, s2, s3, s4)


PARTS_OF = {
    "k2": ((0, 0, 0), (0, 0, 1)),
    "b2": ((1, 0, 0), (1, 0, 1)),
    "r1": ((0, 1, 0), (0, 1, 1)),
    "r2": ((0, 2, 0), (0, 2, 1)),
    "rb1": ((1, 1, 0), (1, 1, 1)),
    "r3": ((0, 3, 0), (0, 3, 1)),
    "r4": ((0, 4, 0),),
    "rb2": ((1, 2, 0), (1, 2, 1)),
    "f3": ((1, 3, 0), (1, 3, 1)),
    "f4": ((1, 4, 0),),
}


def own_parts(*names):
    return tuple(tuple((dx, n, c, 0) for dx, n, c in PARTS_OF[name]) for name in names)


def other_parts(*names):
    return tuple((dx, n, 1 - c, 1) for name in names for dx, n, c in PARTS_OF[name])


EARLY_FROM = own_parts("k2", "b2", "r1", "r2", "rb1") + (other_parts("r1", "r2"),)
LATE_FROM = own_parts("r3", "r4", "rb2", "f3", "f4") + (
    other_parts("rb1", "r3"),
    other_parts("rb2", "r4"),
    other_parts("f3", "f4"),
)


def seq_at(x0, z, core, part):
    dx, steps, other, far_ring = part
    turn = jnp.where((core + far_ring) & 1 == 0, ZS - steps, steps)
    return (((x0 + dx) & 1) * ZS + ((z + turn) & (ZS - 1))) * 2 + ((core + other) & 1)


def add_up(first, *rest):
    total = first.astype(jnp.float32)
    for r in rest:
        total = total + r.astype(jnp.float32)
    return total


def scatter_sums(part, residual):
    p = dict(zip(FEATURE_FROM, part))
    n = residual.shape[0] // 2
    bf = jnp.bfloat16
    far = x_flip(p[(2, 1)])
    from_low = y_up(p[(1, 1)])
    from_high = y_down(p[(-1, 1)])
    c = add_up(p[(2, 0)], far).astype(bf)
    c_low = y_up(c[:n])
    c_high = y_down(c[n:])
    rx = x_flip(add_up(p[(0, 1)], from_low, from_high).astype(bf))
    up = p[(1, 0)]
    down = p[(-1, 0)]
    up = jnp.concatenate([add_up(up[:n], c_low).astype(bf), up[n:]], axis=0)
    down = jnp.concatenate([down[:n], add_up(down[n:], c_high).astype(bf)], axis=0)
    ru = y_up(up)
    rd = y_down(down)
    return add_up(residual, p[(0, 0)], rx, ru, rd).astype(bf)


def dot_f32(a, b):
    return jnp.dot(a, b, preferred_element_type=jnp.float32)


def seq_place():
    return tuple(lax.axis_index(a) for a in SEQ)


def first_block_here():
    x0, z, core = seq_place()
    return ((x0 * ZS + z) * 2 + core) * QB


def head_at(part):
    y, xh = lax.axis_index("head_0"), lax.axis_index("head_1")
    dy, dx = part
    return ((y + dy + YS) & (YS - 1)) * XS + ((xh + dx) & (XS - 1))


def fetch_features(refs, xbuf, sems):
    n = 0
    copies = []
    for k, part in enumerate(FEATURE_FROM):
        place = xbuf.at[head_at(part)]
        pieces = [(refs[k], place)] if k < 6 else [
            (refs[2 * k - 6 + half], place.at[pl.ds(half * HALF, HALF), :]) for half in range(2)
        ]
        for source, target in pieces:
            c = pltpu.make_async_copy(source, target, sems.at[n])
            c.start()
            copies.append(c)
            n += 1
    for c in copies:
        c.wait()


def project(xbuf, gain_ref, rows, weights, sums, squares):
    squares[...] = jnp.zeros_like(squares)
    for a in sums:
        a[...] = jnp.zeros_like(a)

    def block(h, _):
        x = xbuf[h, rows, :].astype(jnp.float32)
        x2 = x * x
        squares[...] += sum(x2[:, c * 128 : (c + 1) * 128] for c in range(4))
        scaled = (x * gain_ref[pl.ds(h, 1), :]).astype(jnp.bfloat16)
        span = pl.ds(pl.multiple_of(h * 512, 512), 512)
        for a, w in zip(sums, weights):
            a[...] += dot_f32(scaled, w[span, :])
        return 0

    lax.fori_loop(0, 8, block, 0)
    total = jnp.sum(squares[...], axis=1, keepdims=True)
    return lax.rsqrt(total * (1.0 / MODEL_WIDTH) + EPSILON)


def rope(u, cos, sin):
    return u * cos + pltpu.roll(u, 64, 1) * sin


def kv_kernel(gain_ref, cos_ref, sin_ref, *refs):
    x_refs, (wk_ref, wv_ref, out_ref, xbuf, k_sum, v_sum, squares, sems) = refs[:10], refs[10:]
    fetch_features(x_refs, xbuf, sems)

    def body(half, _):
        rows = pl.ds(pl.multiple_of(half * HALF, HALF), HALF)
        scale = project(xbuf, gain_ref, rows, (wk_ref, wv_ref), (k_sum, v_sum), squares)
        out_ref[rows, :128] = rope(
            k_sum[...] * scale, cos_ref[rows, :], sin_ref[rows, :]
        ).astype(jnp.bfloat16)
        out_ref[rows, 128:] = (v_sum[...] * scale).astype(jnp.bfloat16)
        return 0

    lax.fori_loop(0, 2, body, 0)


def q_kernel(gain_ref, dil_ref, width_ref, cos_ref, sin_ref, *refs):
    x_refs, (wq_ref, out_ref, list_ref, xbuf, q_sum, squares, sems) = refs[:10], refs[10:]
    fetch_features(x_refs, xbuf, sems)
    x0, z, core = seq_place()
    first = first_block_here()
    side = jnp.where(core == 0, ZS - 1, 1)

    def is_early(b):
        owner = b >> 2
        dz = ((owner >> 1) - z) & (ZS - 1)
        same = (owner >> 4) == x0
        near = jnp.where(((dz + 2) & (ZS - 1)) <= 4, 1, 0)
        across = jnp.where((dz == 0) | (dz == side), 1, 0)
        return jnp.where(same, near, across)

    def lists_of(j, _):
        i = first + j
        low = i - width_ref[j] + 1
        start = jnp.maximum(low, 0)

        def listed(t, counts):
            early, late = counts
            far = t < DILATION_COUNT
            b = jnp.where(
                far, dil_ref[i, jnp.minimum(t, DILATION_COUNT - 1)], start + t - DILATION_COUNT
            )
            list_ref[j, 1 + early] = b
            list_ref[j, LATE + 1 + late] = b
            valid = jnp.where(far & (b >= low), 0, 1)
            e = is_early(b)
            return early + valid * e, late + valid * (1 - e)

        early, late = lax.fori_loop(
            0, i - start + DILATION_COUNT, listed, (jnp.int32(0), jnp.int32(0))
        )
        list_ref[j, 0] = early
        list_ref[j, LATE] = late
        return 0

    lax.fori_loop(0, QB, lists_of, 0)

    def body(half, _):
        rows = pl.ds(pl.multiple_of(half * HALF, HALF), HALF)
        scale = project(xbuf, gain_ref, rows, (wq_ref,), (q_sum,), squares) * SCORE_FACTOR
        for g in range(4):
            cols = slice(g * 128, (g + 1) * 128)
            out_ref[rows, cols] = rope(
                q_sum[:, cols] * scale, cos_ref[rows, :], sin_ref[rows, :]
            ).astype(jnp.bfloat16)
        return 0

    lax.fori_loop(0, 2, body, 0)


def fetch(kv_in, sources, buf, sems):
    x0, z, core = seq_place()
    copies = []
    for ref, parts in zip(kv_in, sources):
        for s, part in enumerate(parts):
            dest = pl.multiple_of(seq_at(x0, z, core, part) * ROWS, ROWS)
            c = pltpu.make_async_copy(
                ref.at[pl.ds(s * ROWS, ROWS), :], buf.at[pl.ds(dest, ROWS), :], sems.at[len(copies)]
            )
            c.start()
            copies.append(c)
    return copies


def load(buf, blocks):
    keys, values = [], []
    for b in blocks:
        r = pl.ds(pl.multiple_of(b * BLOCK, BLOCK), BLOCK)
        keys.append(buf[r, :128])
        values.append(buf[r, 128:])
    ones = jnp.ones((GROUP * BLOCK, 128), jnp.bfloat16)
    values = jnp.concatenate(values, axis=0)
    return jnp.concatenate(keys, axis=0), jnp.concatenate([values, ones], axis=1)


def scored(q_ref, j, half, keys):
    rows = pl.ds(pl.multiple_of(j * BLOCK, BLOCK), BLOCK)
    q = jnp.concatenate(
        [
            q_ref[rows, pl.ds(pl.multiple_of((2 * half + c) * 128, 128), 128)]
            for c in range(2)
        ],
        axis=0,
    )
    return lax.dot_general(q, keys, (((1,), (1,)), ((), ())), preferred_element_type=jnp.float32)


def update(q_ref, j, at, buf, blocks, acc, top, limit=None):
    keys, values = load(buf, blocks)

    def one_half(half, _):
        s = scored(q_ref, j, half, keys)
        if limit is not None:
            col = lax.broadcasted_iota(jnp.int32, s.shape, 1)
            s = jnp.where(col < limit, s, NEGATIVE)
        old = top[at, half]
        new = jnp.maximum(old, jnp.max(s, axis=1, keepdims=True))
        fade = jnp.exp2(old - new)
        p = jnp.exp2(s - jnp.concatenate([new] * GROUP, axis=1)).astype(jnp.bfloat16)
        acc[at, half] = acc[at, half] * jnp.concatenate([fade] * 2, axis=1) + dot_f32(p, values)
        top[at, half] = new
        return 0

    lax.fori_loop(0, 2, one_half, 0, unroll=limit is None)


def early_kernel(base, list_ref, q_ref, *refs):
    n = len(EARLY_FROM)
    kv_in, (acc, top, buf, sems) = refs[:n], refs[n:]
    first_block = first_block_here()
    for c in fetch(kv_in, EARLY_FROM, buf, sems):
        c.wait()

    def one_block(at, _):
        j = base + at
        i = first_block + j
        total = list_ref[j, 0]
        rest = lax.rem(total, GROUP)
        keys, values = load(
            buf, [i] + [jnp.where(t < rest, list_ref[j, 1 + t], i) for t in range(GROUP - 1)]
        )
        shape = (2 * BLOCK, GROUP * BLOCK)
        col = lax.broadcasted_iota(jnp.int32, shape, 1)
        row = lax.broadcasted_iota(jnp.int32, shape, 0) & (BLOCK - 1)
        limit = jnp.where(col < BLOCK, row + 1, (1 + rest) * BLOCK)
        for half in range(2):
            s = jnp.where(col < limit, scored(q_ref, j, half, keys), NEGATIVE)
            m = jnp.max(s, axis=1, keepdims=True)
            p = jnp.exp2(s - m).astype(jnp.bfloat16)
            acc[at, half] = dot_f32(p, values)
            top[at, half] = jnp.broadcast_to(m, (2 * BLOCK, 128))

        def step(g, _):
            t = 1 + rest + g * GROUP
            update(q_ref, j, at, buf, [list_ref[j, t + e] for e in range(GROUP)], acc, top)
            return 0

        lax.fori_loop(0, lax.div(total, GROUP), step, 0)
        return 0

    lax.fori_loop(0, QB // 2, one_block, 0)


def late_kernel(base, list_ref, q_ref, acc_ref, top_ref, w_hbm, *refs):
    n = len(LATE_FROM)
    kv_in, out_refs = refs[:n], refs[n : n + 8]
    acc, top, attention, shares, w_ref, buf, sems = refs[n + 8 :]
    copies = fetch(kv_in, LATE_FROM, buf, sems)
    weights = pltpu.make_async_copy(w_hbm, w_ref, sems.at[len(copies)])
    weights.start()
    for source, target in ((acc_ref, acc), (top_ref, top)):
        c = pltpu.make_async_copy(source, target, sems.at[len(copies) + 1])
        c.start()
        copies.append(c)
    for c in copies:
        c.wait()

    def one_block(at, _):
        j = base + at
        total = list_ref[j, LATE]
        rest = lax.rem(total, GROUP)

        @pl.when(rest > 0)
        def _():
            first = list_ref[j, LATE + 1]
            blocks = [first] + [
                jnp.where(t < rest, list_ref[j, LATE + 1 + t], first) for t in range(1, GROUP)
            ]
            update(q_ref, j, at, buf, blocks, acc, top, rest * BLOCK)

        def step(g, _):
            t = LATE + 1 + rest + g * GROUP
            update(q_ref, j, at, buf, [list_ref[j, t + e] for e in range(GROUP)], acc, top)
            return 0

        lax.fori_loop(0, lax.div(total, GROUP), step, 0)
        rows = pl.ds(pl.multiple_of(at * BLOCK, BLOCK), BLOCK)
        for half in range(2):
            a = acc[at, half]
            o = (a[:, :128] / a[:, 128:]).astype(jnp.bfloat16)
            attention[rows, (2 * half) * 128 : (2 * half + 1) * 128] = o[:BLOCK]
            attention[rows, (2 * half + 1) * 128 : (2 * half + 2) * 128] = o[BLOCK:]
        return 0

    lax.fori_loop(0, QB // 2, one_block, 0)
    weights.wait()

    def share(h, _):
        w = w_ref[:, pl.ds(pl.multiple_of(h * 512, 512), 512)]
        shares[h] = dot_f32(attention[...], w).astype(bf16)
        return 0

    lax.fori_loop(0, 8, share, 0)
    copies = []
    for k, o in enumerate(out_refs):
        c = pltpu.make_async_copy(shares.at[head_at(FEATURE_FROM[k])], o, sems.at[k])
        c.start()
        copies.append(c)
    for c in copies:
        c.wait()


VMEM = pl.BlockSpec(memory_space=pltpu.VMEM)
SMEM = pl.BlockSpec(memory_space=pltpu.SMEM)
ANY = pl.BlockSpec(memory_space=pl.ANY)
bf16 = jnp.bfloat16


ACC = (QB // 2, 2, 2 * BLOCK, 256)
TOP = (QB // 2, 2, 2 * BLOCK, 128)


def attend_early(base, lists, q, early):
    return pl.pallas_call(
        functools.partial(early_kernel, base),
        out_shape=[jax.ShapeDtypeStruct(ACC, jnp.float32), jax.ShapeDtypeStruct(TOP, jnp.float32)],
        in_specs=[SMEM, VMEM] + [ANY] * len(early),
        out_specs=[VMEM] * 2,
        scratch_shapes=[pltpu.VMEM((32 * ROWS, 256), bf16), pltpu.SemaphoreType.DMA((32,))],
        cost_estimate=pl.CostEstimate(flops=5 * 10**9, transcendentals=10**6, bytes_accessed=4 * 10**6),
        name="attend_early",
    )(lists, q, *early)


def attend_late(base, lists, q, state, w_output, late):
    return pl.pallas_call(
        functools.partial(late_kernel, base),
        out_shape=[jax.ShapeDtypeStruct((HALF, 512), bf16)] * 8,
        in_specs=[SMEM, VMEM] + [ANY] * (3 + len(late)),
        out_specs=[ANY] * 8,
        scratch_shapes=[
            pltpu.VMEM(ACC, jnp.float32),
            pltpu.VMEM(TOP, jnp.float32),
            pltpu.VMEM((HALF, 512), bf16),
            pltpu.VMEM((8, HALF, 512), bf16),
            pltpu.VMEM((512, MODEL_WIDTH), bf16),
            pltpu.VMEM((32 * ROWS, 256), bf16),
            pltpu.SemaphoreType.DMA((32,)),
        ],
        cost_estimate=pl.CostEstimate(flops=5 * 10**9, transcendentals=10**6, bytes_accessed=10**7),
        name="attend_late",
    )(lists, q, *state, w_output, *late)


def shards(tokens, norm_gain, w_query, w_key, w_value, w_output, widths, dilation):
    half_size = HEAD_WIDTH // 2
    positions = first_block_here() * BLOCK + jnp.arange(ROWS, dtype=jnp.int32)
    frequency = ROPE_BASE ** (-jnp.arange(half_size, dtype=jnp.float32) * 2.0 / HEAD_WIDTH)
    angles = positions.astype(jnp.float32)[:, None] * frequency[None, :]
    cosine, sine = jnp.cos(angles), jnp.sin(angles)
    cosine = jnp.concatenate([cosine, cosine], axis=1)
    sine = jnp.concatenate([-sine, sine], axis=1)
    gain = norm_gain.reshape(8, 512)

    full, quarter = gather_features(tokens)
    pieces = full + quarter
    kv = pl.pallas_call(
        kv_kernel,
        out_shape=jax.ShapeDtypeStruct((ROWS, 256), bf16),
        in_specs=[VMEM] * 3 + [ANY] * 10 + [VMEM] * 2,
        out_specs=VMEM,
        scratch_shapes=[
            pltpu.VMEM((8, ROWS, 512), bf16),
            pltpu.VMEM((HALF, 128), jnp.float32),
            pltpu.VMEM((HALF, 128), jnp.float32),
            pltpu.VMEM((HALF, 128), jnp.float32),
            pltpu.SemaphoreType.DMA((10,)),
        ],
        cost_estimate=pl.CostEstimate(flops=10**9, transcendentals=0, bytes_accessed=6 * 10**6),
        name="keys_values",
    )(gain, cosine, sine, *pieces, w_key, w_value)
    early, late = gather_blocks(kv)
    query_call = pl.pallas_call(
        q_kernel,
        out_shape=[
            jax.ShapeDtypeStruct((ROWS, 512), bf16),
            jax.ShapeDtypeStruct((QB, 2 * LATE), jnp.int32),
        ],
        in_specs=[VMEM] + [SMEM] * 2 + [VMEM] * 2 + [ANY] * 10 + [VMEM],
        out_specs=[VMEM, SMEM],
        scratch_shapes=[
            pltpu.VMEM((8, ROWS, 512), bf16),
            pltpu.VMEM((HALF, 512), jnp.float32),
            pltpu.VMEM((HALF, 128), jnp.float32),
            pltpu.SemaphoreType.DMA((10,)),
        ],
        cost_estimate=pl.CostEstimate(flops=4 * 10**9, transcendentals=0, bytes_accessed=10**7),
        name="queries",
    )
    q, lists = query_call(gain, dilation, widths, cosine, sine, *pieces, w_query)
    states = [attend_early(k * QB // 2, lists, q, early) for k in range(2)]
    outs = []
    for k in range(2):
        shares = attend_late(k * QB // 2, lists, q, states[k], w_output, late)
        outs.append(scatter_sums(shares, tokens[k * HALF : (k + 1) * HALF]))
    return cat(*outs)


def solution(mesh):
    split = Mesh(mesh.devices.reshape(2, ZS, 2, YS, XS), SEQ + HEAD)
    placed = (
        P(SEQ, HEAD),
        P(),
        P(None, HEAD),
        P(None, HEAD),
        P(None, HEAD),
        P(HEAD, None),
        P(SEQ),
        P(),
    )
    return jax.shard_map(
        shards, mesh=split, in_specs=placed, out_specs=P(SEQ, HEAD), check_vma=False
    )
```

time: 190 us -> 202 us (1.063)
  the two profiles are of different devices: /device:TPU:6 before, /device:TPU:2 now
where the time goes in v1:
time: 202 us; the launch traced here: 201 us
  Pallas kernels  72.2 us (36%)
  waiting for transfers between devices  64.6 us (32%)
  starting transfers between devices  48 us (24%)
  other arithmetic  9.46 us (5%)
  local copies, waits for them, and re-layouts  6.4 us (3%)
    ppermute x34, starting transfers between devices, moved(): return lax.ppermute(x, axis, [(k, (k + step) % size) for k in range(size)])  45.8 us
    ppermute x34, waiting for transfers between devices, moved(): return lax.ppermute(x, axis, [(k, (k + step) % size) for k in range(size)])  43.8 us
    pallas_call x2, Pallas kernels, attend_late(): pl.pallas_call(functools.partial(late_kernel, base), out_shape=[jax.Shape...  32.1 us
    ppermute x6, waiting for transfers between devices, ring(): return lax.ppermute(x, ('seq_1', 'seq_2'), pairs)  20.8 us
    pallas_call x2, Pallas kernels, attend_early(): pl.pallas_call(functools.partial(early_kernel, base), out_shape=[jax.Shap...  18.2 us
    pallas_call x1, Pallas kernels, shards(): query_call(gain, dilation, widths, cosine, sine, *pieces, w_query)  12.1 us
    pallas_call x1, Pallas kernels, shards(): pl.pallas_call(kv_kernel, out_shape=jax.ShapeDtypeStruct((ROWS, 256), bf1...  9.8 us
    concatenate x5, other arithmetic, cat(): return jnp.concatenate(v, axis=0)  4.36 us
  transfers between devices with their start and end apart: 40, of which 17 were waited for; matrix products, arithmetic and copies ran while one was open for 6% of the time, Pallas kernels for 23%

profile of v1, /device:TPU:2, one launch (start us, length us, event | category | flops | bytes accessed | tf_op | source)
XLA Modules:
  0.0 201.2 jit_solution(11496322119037599125)
XLA Ops:
  5.4 9.8 %collective-permute-done.1.refs_2_ = bf16[512,512]{1,0:T(8,128)(2,1)S(1)} collective-permute-done((bf16[512,512]{1,0:T(8,128)(2,1)}, bf16[512,512]{1,0:T(8,128)(2,1)S(1)}, u32[]{:S(2)}, u32[]{:S(2)}) %collective-permute-start.1) | collective-permute-done | bytes 524320 | tf_op jit(solution)/shard_map/ppermute | solution.py:31
  16.3 2.9 %collective-permute-start.6 = (bf16[256,512]{1,0:T(8,128)(2,1)}, bf16[256,512]{1,0:T(8,128)(2,1)S(1)}, u32[]{:S(2)}, u32[]{:S(2)}) collective-permute-start(bf16[256,512]{1,0:T(8,128)(2,1)} %slice.69), channel_id=1, source_target_pairs={{0,6},{2,0},{4,2},{6,4},{1,7},{3,1},{5,3},{7,5},{8,14},{10,8},{12,... | collective-permute-start | bytes 786440 | tf_op jit(solution)/shard_map/ppermute | solution.py:31
  19.2 3.2 %collective-permute-start.4 = (bf16[512,512]{1,0:T(8,128)(2,1)S(1)}, bf16[512,512]{1,0:T(8,128)(2,1)S(1)}, u32[]{:S(2)}, u32[]{:S(2)}) collective-permute-start(bf16[512,512]{1,0:T(8,128)(2,1)S(1)} %collective-permute-done.refs_1_), channel_id=1, source_target_pairs={{0,6},{2,0},{4,2},{6,4},{1,7},{3,1},{5,3},{7,5},{8,14},{10,8},{12,... | collective-permute-start | bytes 1572872 | tf_op jit(solution)/shard_map/ppermute | solution.py:31
  31.2 3.3 %collective-permute-done.7.refs_8_ = bf16[256,512]{1,0:T(8,128)(2,1)S(1)} collective-permute-done((bf16[256,512]{1,0:T(8,128)(2,1)S(1)}, bf16[256,512]{1,0:T(8,128)(2,1)S(1)}, u32[]{:S(2)}, u32[]{:S(2)}) %collective-permute-start.7) | collective-permute-done | bytes 262176 | tf_op jit(solution)/shard_map/ppermute | solution.py:31
  34.4 2.8 %collective-permute-done.8.refs_9_ = bf16[256,512]{1,0:T(8,128)(2,1)S(1)} collective-permute-done((bf16[256,512]{1,0:T(8,128)(2,1)S(1)}, bf16[256,512]{1,0:T(8,128)(2,1)S(1)}, u32[]{:S(2)}, u32[]{:S(2)}) %collective-permute-start.8) | collective-permute-done | bytes 262176 | tf_op jit(solution)/shard_map/ppermute | solution.py:31
  38.7 9.8 %keys_values.1 = bf16[512,256]{1,0:T(8,128)(2,1)} custom-call(f32[8,512]{1,0:T(8,128)} %reshape.14.gain_ref, f32[512,128]{1,0:T(8,128)} %get-tuple-element.58.cos_ref, f32[512,128]{1,0:T(8,128)} %get-tuple-element.59.sin_ref, bf16[512,512]{1,0:T(8,128)(2,1)} %refs_0_.3, bf16[512,512]{1,0:T(8,128)(2,1)} %copy-done.4, bf16[512,512]{1,0:T(8,128)(2,1)} %copy-done.1, ...), custom_call_target="tpu_custom_call" | custom-call | flops 1000000000 | bytes 6000000 | tf_op jit(solution)/shard_map/keys_values/pallas_call | solution.py:502
  53.9 6.0 %collective-permute-done.10 = bf16[512,256]{1,0:T(8,128)(2,1)S(1)} collective-permute-done((bf16[512,256]{1,0:T(8,128)(2,1)}, bf16[512,256]{1,0:T(8,128)(2,1)S(1)}, u32[]{:S(2)}, u32[]{:S(2)}) %collective-permute-start.10) | collective-permute-done | bytes 262176 | tf_op jit(solution)/shard_map/ppermute | solution.py:31
  60.0 2.9 %collective-permute-start.11 = (bf16[512,256]{1,0:T(8,128)(2,1)S(1)}, bf16[512,256]{1,0:T(8,128)(2,1)S(1)}, u32[]{:S(2)}, u32[]{:S(2)}) collective-permute-start(bf16[512,256]{1,0:T(8,128)(2,1)S(1)} %collective-permute-done.10), channel_id=1, source_target_pairs={{0,8},{8,0},{1,9},{9,1},{2,10},{10,2},{3,11},{11,3},{4,12},{12,4},... | collective-permute-start | bytes 786440 | tf_op jit(solution)/shard_map/ppermute | solution.py:31
  64.7 10.2 %collective-permute-done.13.refs_3_ = bf16[1024,256]{1,0:T(8,128)(2,1)S(1)} collective-permute-done((bf16[1024,256]{1,0:T(8,128)(2,1)S(1)}, bf16[1024,256]{1,0:T(8,128)(2,1)S(1)}, u32[]{:S(2)}, u32[]{:S(2)}) %collective-permute-start.13) | collective-permute-done | bytes 524320 | tf_op jit(solution)/shard_map/ppermute | solution.py:76
  75.7 4.8 %collective-permute-done.14.refs_4_ = bf16[1024,256]{1,0:T(8,128)(2,1)S(1)} collective-permute-done((bf16[1024,256]{1,0:T(8,128)(2,1)S(1)}, bf16[1024,256]{1,0:T(8,128)(2,1)S(1)}, u32[]{:S(2)}, u32[]{:S(2)}) %collective-permute-start.14) | collective-permute-done | bytes 524320 | tf_op jit(solution)/shard_map/ppermute | solution.py:76
  81.9 4.2 %collective-permute-done.16.refs_0_ = bf16[1024,256]{1,0:T(8,128)(2,1)S(1)} collective-permute-done((bf16[1024,256]{1,0:T(8,128)(2,1)S(1)}, bf16[1024,256]{1,0:T(8,128)(2,1)S(1)}, u32[]{:S(2)}, u32[]{:S(2)}) %collective-permute-start.16) | collective-permute-done | bytes 524320 | tf_op jit(solution)/shard_map/ppermute | solution.py:76
  86.9 12.1 %queries.1 = (bf16[512,512]{1,0:T(8,128)(2,1)}, s32[4,128]{1,0:T(4,128)}) custom-call(f32[8,512]{1,0:T(8,128)} %reshape.14.gain_ref, s32[128,8]{1,0:T(8,128)} %copy.9.dil_ref, s32[4]{0:T(128)} %width_ref.1, f32[512,128]{1,0:T(8,128)} %get-tuple-element.58.cos_ref, f32[512,128]{1,0:T(8,128)} %get-tuple-element.59.sin_ref, bf16[512,512]{1,0:T(8,128)(2,1)} %refs_0_.3, ...), custom_call_target="tpu_custom_call" | custom-call | flops 4000000000 | bytes 10000000 | tf_op jit(solution)/shard_map/queries/pallas_call | solution.py:535
  101.6 6.8 %collective-permute-done.20.refs_4_ = bf16[512,256]{1,0:T(8,128)(2,1)S(1)} collective-permute-done((bf16[512,256]{1,0:T(8,128)(2,1)}, bf16[512,256]{1,0:T(8,128)(2,1)S(1)}, u32[]{:S(2)}, u32[]{:S(2)}) %collective-permute-start.20) | collective-permute-done | bytes 262176 | tf_op jit(solution)/shard_map/ppermute | solution.py:31
  110.4 9.5 %attend_early.3 = (f32[2,2,256,256]{3,2,1,0:T(8,128)}, f32[2,2,256,128]{3,2,1,0:T(8,128)}) custom-call(s32[4,128]{1,0:T(4,128)} %get-tuple-element.27.list_ref, bf16[512,512]{1,0:T(8,128)(2,1)} %get-tuple-element.28.q_ref, bf16[1024,256]{1,0:T(8,128)(2,1)} %copy-done.7, bf16[1024,256]{1,0:T(8,128)(2,1)} %copy-done.26, bf16[1024,256]{1,0:T(8,128)(2,1)} %copy-done.8, ...), custom_call_target="tpu_custom_call" | custom-call | flops 5000000000 | bytes 4000000 | tf_op jit(solution)/shard_map/attend_early/pallas_call | solution.py:459
  119.9 8.7 %attend_early.2 = (f32[2,2,256,256]{3,2,1,0:T(8,128)}, f32[2,2,256,128]{3,2,1,0:T(8,128)}) custom-call(s32[4,128]{1,0:T(4,128)} %get-tuple-element.27.list_ref, bf16[512,512]{1,0:T(8,128)(2,1)} %get-tuple-element.28.q_ref, bf16[1024,256]{1,0:T(8,128)(2,1)} %copy-done.7, bf16[1024,256]{1,0:T(8,128)(2,1)} %copy-done.26, bf16[1024,256]{1,0:T(8,128)(2,1)} %copy-done.8, ...), custom_call_target="tpu_custom_call" | custom-call | flops 5000000000 | bytes 4000000 | tf_op jit(solution)/shard_map/attend_early/pallas_call | solution.py:459
  128.7 15.6 %attend_late.3 = (bf16[256,512]{1,0:T(8,128)(2,1)}, bf16[256,512]{1,0:T(8,128)(2,1)}, bf16[256,512]{1,0:T(8,128)(2,1)}, bf16[256,512]{1,0:T(8,128)(2,1)}, bf16[2...) custom-call(s32[4,128]{1,0:T(4,128)} %get-tuple-element.27.list_ref, ...), custom_call_target="tpu_custom_call" | custom-call | flops 5000000000 | bytes 10000000 | tf_op jit(solution)/shard_map/attend_late/pallas_call | solution.py:471
  144.4 3.2 %collective-permute-start.33 = (bf16[256,512]{1,0:T(8,128)(2,1)}, bf16[256,512]{1,0:T(8,128)(2,1)S(1)}, u32[]{:S(2)}, u32[]{:S(2)}) collective-permute-start(bf16[256,512]{1,0:T(8,128)(2,1)} %get-tuple-element.44), channel_id=1, source_target_pairs={{0,6},{2,0},{4,2},{6,4},{1,7},{3,1},{5,3},{7,5},{8,14},{10,8},{12,... | collective-permute-start | bytes 786440 | tf_op jit(solution)/shard_map/ppermute | solution.py:31
  147.7 2.4 %collective-permute-start.35 = (bf16[256,512]{1,0:T(8,128)(2,1)}, bf16[256,512]{1,0:T(8,128)(2,1)S(1)}, u32[]{:S(2)}, u32[]{:S(2)}) collective-permute-start(bf16[256,512]{1,0:T(8,128)(2,1)} %get-tuple-element.47), channel_id=1, source_target_pairs={{0,1},{1,0},{2,3},{3,2},{4,5},{5,4},{6,7},{7,6},{8,9},{9,8},{10,11... | collective-permute-start | bytes 786440 | tf_op jit(solution)/shard_map/ppermute | solution.py:31
  150.1 16.5 %attend_late.2 = (bf16[256,512]{1,0:T(8,128)(2,1)}, bf16[256,512]{1,0:T(8,128)(2,1)}, bf16[256,512]{1,0:T(8,128)(2,1)}, bf16[256,512]{1,0:T(8,128)(2,1)}, bf16[2...) custom-call(s32[4,128]{1,0:T(4,128)} %get-tuple-element.27.list_ref, ...), custom_call_target="tpu_custom_call" | custom-call | flops 5000000000 | bytes 10000000 | tf_op jit(solution)/shard_map/attend_late/pallas_call | solution.py:471
  166.7 3.2 %collective-permute-start.25 = (bf16[256,512]{1,0:T(8,128)(2,1)}, bf16[256,512]{1,0:T(8,128)(2,1)S(1)}, u32[]{:S(2)}, u32[]{:S(2)}) collective-permute-start(bf16[256,512]{1,0:T(8,128)(2,1)} %get-tuple-element.34), channel_id=1, source_target_pairs={{0,6},{2,0},{4,2},{6,4},{1,7},{3,1},{5,3},{7,5},{8,14},{10,8},{12,... | collective-permute-start | bytes 786440 | tf_op jit(solution)/shard_map/ppermute | solution.py:31
  173.1 2.5 %collective-permute-start.34 = (bf16[256,512]{1,0:T(8,128)(2,1)S(1)}, bf16[256,512]{1,0:T(8,128)(2,1)S(1)}, u32[]{:S(2)}, u32[]{:S(2)}) collective-permute-start(bf16[256,512]{1,0:T(8,128)(2,1)S(1)} %add_convert_fusion.2), channel_id=1, source_target_pairs={{0,1},{1,0},{2,3},{3,2},{4,5},{5,4},{6,7},{7,6},{8,9},{9,8},{10,11... | collective-permute-start | bytes 786440 | tf_op jit(solution)/shard_map/ppermute | solution.py:31
  175.8 3.2 %collective-permute-start.38 = (bf16[128,512]{1,0:T(8,128)(2,1)S(1)}, bf16[128,512]{1,0:T(8,128)(2,1)S(1)}, u32[]{:S(2)}, u32[]{:S(2)}) collective-permute-start(bf16[128,512]{1,0:T(8,128)(2,1)S(1)} %get-tuple-element.54), channel_id=1, source_target_pairs={{0,6},{2,0},{4,2},{6,4},{1,7},{3,1},{5,3},{7,5},{8,14},{10,8},{12,... | collective-permute-start | bytes 393224 | tf_op jit(solution)/shard_map/ppermute | solution.py:31
  183.3 3.0 %collective-permute-start.30 = (bf16[128,512]{1,0:T(8,128)(2,1)S(1)}, bf16[128,512]{1,0:T(8,128)(2,1)S(1)}, u32[]{:S(2)}, u32[]{:S(2)}) collective-permute-start(bf16[128,512]{1,0:T(8,128)(2,1)S(1)} %get-tuple-element.52), channel_id=1, source_target_pairs={{0,6},{2,0},{4,2},{6,4},{1,7},{3,1},{5,3},{7,5},{8,14},{10,8},{12,... | collective-permute-start | bytes 393224 | tf_op jit(solution)/shard_map/ppermute | solution.py:31
  186.5 4.1 %collective-permute-done.28 = bf16[128,512]{1,0:T(8,128)(2,1)S(1)} collective-permute-done((bf16[128,512]{1,0:T(8,128)(2,1)S(1)}, bf16[128,512]{1,0:T(8,128)(2,1)S(1)}, u32[]{:S(2)}, u32[]{:S(2)}) %collective-permute-start.28) | collective-permute-done | bytes 131104 | tf_op jit(solution)/shard_map/ppermute | solution.py:31
  (154 shorter events, 49.8 us)
Async XLA Ops:
  0.0 15.1 %collective-permute-start.1 = (bf16[512,512]{1,0:T(8,128)(2,1)}, bf16[512,512]{1,0:T(8,128)(2,1)S(1)}, u32[]{:S(2)}, u32[]{:S(2)}) collective-permute-start(bf16[512,512]{1,0:T(8,128)(2,1)} %refs_0_.3), channel_id=1, source_target_pairs={{0,2},{2,4},{4,6},{6,0},{1,3},{3,5},{5,7},{7,1},{8,10},{10,12},{12... | collective-permute-start | bytes 1572872 | tf_op jit(solution)/shard_map/ppermute | solution.py:31
  1.6 14.0 %collective-permute-start.2 = (bf16[512,512]{1,0:T(8,128)(2,1)}, bf16[512,512]{1,0:T(8,128)(2,1)S(1)}, u32[]{:S(2)}, u32[]{:S(2)}) collective-permute-start(bf16[512,512]{1,0:T(8,128)(2,1)} %refs_0_.3), channel_id=1, source_target_pairs={{0,6},{2,0},{4,2},{6,4},{1,7},{3,1},{5,3},{7,5},{8,14},{10,8},{12,... | collective-permute-start | bytes 1572872 | tf_op jit(solution)/shard_map/ppermute | solution.py:31
  3.2 16.0 %collective-permute-start = (bf16[512,512]{1,0:T(8,128)(2,1)}, bf16[512,512]{1,0:T(8,128)(2,1)S(1)}, u32[]{:S(2)}, u32[]{:S(2)}) collective-permute-start(bf16[512,512]{1,0:T(8,128)(2,1)} %refs_0_.3), channel_id=1, source_target_pairs={{0,1},{1,0},{2,3},{3,2},{4,5},{5,4},{6,7},{7,6},{8,9},{9,8},{10,11... | collective-permute-start | bytes 1572872 | tf_op jit(solution)/shard_map/ppermute | solution.py:31
  16.3 11.5 %collective-permute-start.6 = (bf16[256,512]{1,0:T(8,128)(2,1)}, bf16[256,512]{1,0:T(8,128)(2,1)S(1)}, u32[]{:S(2)}, u32[]{:S(2)}) collective-permute-start(bf16[256,512]{1,0:T(8,128)(2,1)} %slice.69), channel_id=1, source_target_pairs={{0,6},{2,0},{4,2},{6,4},{1,7},{3,1},{5,3},{7,5},{8,14},{10,8},{12,... | collective-permute-start | bytes 786440 | tf_op jit(solution)/shard_map/ppermute | solution.py:31
  19.2 18.0 %collective-permute-start.3 = (bf16[512,512]{1,0:T(8,128)(2,1)S(1)}, bf16[512,512]{1,0:T(8,128)(2,1)S(1)}, u32[]{:S(2)}, u32[]{:S(2)}) collective-permute-start(bf16[512,512]{1,0:T(8,128)(2,1)S(1)} %collective-permute-done.refs_1_), channel_id=1, source_target_pairs={{0,2},{2,4},{4,6},{6,0},{1,3},{3,5},{5,7},{7,1},{8,10},{10,12},{12... | collective-permute-start | bytes 1572872 | tf_op jit(solution)/shard_map/ppermute | solution.py:31
  19.2 18.0 %collective-permute-start.4 = (bf16[512,512]{1,0:T(8,128)(2,1)S(1)}, bf16[512,512]{1,0:T(8,128)(2,1)S(1)}, u32[]{:S(2)}, u32[]{:S(2)}) collective-permute-start(bf16[512,512]{1,0:T(8,128)(2,1)S(1)} %collective-permute-done.refs_1_), channel_id=1, source_target_pairs={{0,6},{2,0},{4,2},{6,4},{1,7},{3,1},{5,3},{7,5},{8,14},{10,8},{12,... | collective-permute-start | bytes 1572872 | tf_op jit(solution)/shard_map/ppermute | solution.py:31
  51.4 13.1 %collective-permute-start.12 = (bf16[1024,256]{1,0:T(8,128)(2,1)S(1)}, bf16[1024,256]{1,0:T(8,128)(2,1)S(1)}, u32[]{:S(2)}, u32[]{:S(2)}) collective-permute-start(bf16[1024,256]{1,0:T(8,128)(2,1)S(1)} %pad_maximum_fusion.4.refs_0_), channel_id=1, source_target_pairs={{0,16},{8,120},{16,32},{24,8},{32,48},{40,24},{48,64},{56,40},{64,... | collective-permute-start | bytes 1572872 | tf_op jit(solution)/shard_map/ppermute | solution.py:76
  64.6 15.9 %collective-permute-start.14 = (bf16[1024,256]{1,0:T(8,128)(2,1)S(1)}, bf16[1024,256]{1,0:T(8,128)(2,1)S(1)}, u32[]{:S(2)}, u32[]{:S(2)}) collective-permute-start(bf16[1024,256]{1,0:T(8,128)(2,1)S(1)} %constant_dynamic-update-slice_fusion.refs_1_), channel_id=1, source_target_pairs={{0,16},{8,120},{16,32},{24,8},{32,48},{40,24},{48,64},{56,40},{64,... | collective-permute-start | bytes 1572872 | tf_op jit(solution)/shard_map/ppermute | solution.py:76
  74.9 11.2 %collective-permute-start.16 = (bf16[1024,256]{1,0:T(8,128)(2,1)S(1)}, bf16[1024,256]{1,0:T(8,128)(2,1)S(1)}, u32[]{:S(2)}, u32[]{:S(2)}) collective-permute-start(bf16[1024,256]{1,0:T(8,128)(2,1)S(1)} %collective-permute-done.13.refs_3_), channel_id=1, source_target_pairs={{0,16},{8,120},{16,32},{24,8},{32,48},{40,24},{48,64},{56,40},{64,... | collective-permute-start | bytes 1572872 | tf_op jit(solution)/shard_map/ppermute | solution.py:76
  80.5 19.8 %collective-permute-start.18 = (bf16[1024,256]{1,0:T(8,128)(2,1)S(1)}, bf16[1024,256]{1,0:T(8,128)(2,1)}, u32[]{:S(2)}, u32[]{:S(2)}) collective-permute-start(bf16[1024,256]{1,0:T(8,128)(2,1)S(1)} %collective-permute-done.14.refs_4_), channel_id=1, source_target_pairs={{0,16},{8,120},{16,32},{24,8},{32,48},{40,24},{48,64},{56,40},{64,... | collective-permute-start | bytes 1572872 | tf_op jit(solution)/shard_map/ppermute | solution.py:76
  80.6 29.8 %collective-permute-start.15 = (bf16[2048,256]{1,0:T(8,128)(2,1)S(1)}, bf16[2048,256]{1,0:T(8,128)(2,1)}, u32[]{:S(2)}, u32[]{:S(2)}) collective-permute-start(bf16[2048,256]{1,0:T(8,128)(2,1)S(1)} %pad_maximum_fusion), channel_id=1, source_target_pairs={{0,8},{8,0},{1,9},{9,1},{2,10},{10,2},{3,11},{11,3},{4,12},{12,4},... | collective-permute-start | bytes 3145736 | tf_op jit(solution)/shard_map/ppermute | solution.py:31
  86.1 12.9 %collective-permute-start.17 = (bf16[512,256]{1,0:T(8,128)(2,1)S(1)}, bf16[512,256]{1,0:T(8,128)(2,1)}, u32[]{:S(2)}, u32[]{:S(2)}) collective-permute-start(bf16[512,256]{1,0:T(8,128)(2,1)S(1)} %slice.70), channel_id=1, source_target_pairs={{0,16},{8,120},{16,32},{24,8},{32,48},{40,24},{48,64},{56,40},{64,... | collective-permute-start | bytes 786440 | tf_op jit(solution)/shard_map/ppermute | solution.py:76
  86.2 22.1 %collective-permute-start.19 = (bf16[1024,256]{1,0:T(8,128)(2,1)S(1)}, bf16[1024,256]{1,0:T(8,128)(2,1)}, u32[]{:S(2)}, u32[]{:S(2)}) collective-permute-start(bf16[1024,256]{1,0:T(8,128)(2,1)S(1)} %collective-permute-done.16.refs_0_), channel_id=1, source_target_pairs={{0,128},{128,0},{1,129},{129,1},{2,130},{130,2},{3,131},{131,3},{4... | collective-permute-start | bytes 1572872 | tf_op jit(solution)/shard_map/ppermute | solution.py:31
  99.7 29.0 %collective-permute-start.21 = (bf16[2048,256]{1,0:T(8,128)(2,1)S(1)}, bf16[2048,256]{1,0:T(8,128)(2,1)}, u32[]{:S(2)}, u32[]{:S(2)}) collective-permute-start(bf16[2048,256]{1,0:T(8,128)(2,1)S(1)} %pad_maximum_fusion.1), channel_id=1, source_target_pairs={{0,8},{8,0},{1,9},{9,1},{2,10},{10,2},{3,11},{11,3},{4,12},{12,4},... | collective-permute-start | bytes 3145736 | tf_op jit(solution)/shard_map/ppermute | solution.py:31
  101.5 27.2 %collective-permute-start.22 = (bf16[1536,256]{1,0:T(8,128)(2,1)S(1)}, bf16[1536,256]{1,0:T(8,128)(2,1)}, u32[]{:S(2)}, u32[]{:S(2)}) collective-permute-start(bf16[1536,256]{1,0:T(8,128)(2,1)S(1)} %pad_maximum_fusion.2), channel_id=1, source_target_pairs={{0,8},{8,0},{1,9},{9,1},{2,10},{10,2},{3,11},{11,3},{4,12},{12,4},... | collective-permute-start | bytes 2359304 | tf_op jit(solution)/shard_map/ppermute | solution.py:31
  110.4 18.3 %collective-permute-start.23 = (bf16[1536,256]{1,0:T(8,128)(2,1)}, bf16[1536,256]{1,0:T(8,128)(2,1)}, u32[]{:S(2)}, u32[]{:S(2)}) collective-permute-start(bf16[1536,256]{1,0:T(8,128)(2,1)} %pad_maximum_fusion.3), channel_id=1, source_target_pairs={{0,8},{8,0},{1,9},{9,1},{2,10},{10,2},{3,11},{11,3},{4,12},{12,4},... | collective-permute-start | bytes 2359304 | tf_op jit(solution)/shard_map/ppermute | solution.py:31
  144.3 27.4 %collective-permute-start.32 = (bf16[256,512]{1,0:T(8,128)(2,1)}, bf16[256,512]{1,0:T(8,128)(2,1)S(1)}, u32[]{:S(2)}, u32[]{:S(2)}) collective-permute-start(bf16[256,512]{1,0:T(8,128)(2,1)} %get-tuple-element.43), channel_id=1, source_target_pairs={{0,2},{2,4},{4,6},{6,0},{1,3},{3,5},{5,7},{7,1},{8,10},{10,12},{12... | collective-permute-start | bytes 786440 | tf_op jit(solution)/shard_map/ppermute | solution.py:31
  144.4 28.6 %collective-permute-start.33 = (bf16[256,512]{1,0:T(8,128)(2,1)}, bf16[256,512]{1,0:T(8,128)(2,1)S(1)}, u32[]{:S(2)}, u32[]{:S(2)}) collective-permute-start(bf16[256,512]{1,0:T(8,128)(2,1)} %get-tuple-element.44), channel_id=1, source_target_pairs={{0,6},{2,0},{4,2},{6,4},{1,7},{3,1},{5,3},{7,5},{8,14},{10,8},{12,... | collective-permute-start | bytes 786440 | tf_op jit(solution)/shard_map/ppermute | solution.py:31
  147.7 27.9 %collective-permute-start.35 = (bf16[256,512]{1,0:T(8,128)(2,1)}, bf16[256,512]{1,0:T(8,128)(2,1)S(1)}, u32[]{:S(2)}, u32[]{:S(2)}) collective-permute-start(bf16[256,512]{1,0:T(8,128)(2,1)} %get-tuple-element.47), channel_id=1, source_target_pairs={{0,1},{1,0},{2,3},{3,2},{4,5},{5,4},{6,7},{7,6},{8,9},{9,8},{10,11... | collective-permute-start | bytes 786440 | tf_op jit(solution)/shard_map/ppermute | solution.py:31
  166.7 12.3 %collective-permute-start.25 = (bf16[256,512]{1,0:T(8,128)(2,1)}, bf16[256,512]{1,0:T(8,128)(2,1)S(1)}, u32[]{:S(2)}, u32[]{:S(2)}) collective-permute-start(bf16[256,512]{1,0:T(8,128)(2,1)} %get-tuple-element.34), channel_id=1, source_target_pairs={{0,6},{2,0},{4,2},{6,4},{1,7},{3,1},{5,3},{7,5},{8,14},{10,8},{12,... | collective-permute-start | bytes 786440 | tf_op jit(solution)/shard_map/ppermute | solution.py:31
  171.8 11.0 %collective-permute-start.27 = (bf16[256,512]{1,0:T(8,128)(2,1)}, bf16[256,512]{1,0:T(8,128)(2,1)S(1)}, u32[]{:S(2)}, u32[]{:S(2)}) collective-permute-start(bf16[256,512]{1,0:T(8,128)(2,1)} %get-tuple-element.37), channel_id=1, source_target_pairs={{0,1},{1,0},{2,3},{3,2},{4,5},{5,4},{6,7},{7,6},{8,9},{9,8},{10,11... | collective-permute-start | bytes 786440 | tf_op jit(solution)/shard_map/ppermute | solution.py:31
  173.1 20.4 %collective-permute-start.34 = (bf16[256,512]{1,0:T(8,128)(2,1)S(1)}, bf16[256,512]{1,0:T(8,128)(2,1)S(1)}, u32[]{:S(2)}, u32[]{:S(2)}) collective-permute-start(bf16[256,512]{1,0:T(8,128)(2,1)S(1)} %add_convert_fusion.2), channel_id=1, source_target_pairs={{0,1},{1,0},{2,3},{3,2},{4,5},{5,4},{6,7},{7,6},{8,9},{9,8},{10,11... | collective-permute-start | bytes 786440 | tf_op jit(solution)/shard_map/ppermute | solution.py:31
  175.8 10.5 %collective-permute-start.38 = (bf16[128,512]{1,0:T(8,128)(2,1)S(1)}, bf16[128,512]{1,0:T(8,128)(2,1)S(1)}, u32[]{:S(2)}, u32[]{:S(2)}) collective-permute-start(bf16[128,512]{1,0:T(8,128)(2,1)S(1)} %get-tuple-element.54), channel_id=1, source_target_pairs={{0,6},{2,0},{4,2},{6,4},{1,7},{3,1},{5,3},{7,5},{8,14},{10,8},{12,... | collective-permute-start | bytes 393224 | tf_op jit(solution)/shard_map/ppermute | solution.py:31
  179.9 14.9 %collective-permute-start.26 = (bf16[256,512]{1,0:T(8,128)(2,1)}, bf16[256,512]{1,0:T(8,128)(2,1)S(1)}, u32[]{:S(2)}, u32[]{:S(2)}) collective-permute-start(bf16[256,512]{1,0:T(8,128)(2,1)} %add_convert_fusion.5), channel_id=1, source_target_pairs={{0,1},{1,0},{2,3},{3,2},{4,5},{5,4},{6,7},{7,6},{8,9},{9,8},{10,11... | collective-permute-start | bytes 786440 | tf_op jit(solution)/shard_map/ppermute | solution.py:31
  (44 other events, 533.1 us)

commit v2 on v0

--- a/solution.py
+++ b/solution.py
@@ -248,10 +248,17 @@
     lax.fori_loop(0, 2, body, 0)
 
 
-def out_kernel(which, at_ref, w_ref, *out_refs):
-    for k, o in zip(which, out_refs):
+def out_kernel(which, at_ref, w_hbm, *refs):
+    out_refs, (w_ref, sems) = refs[: len(which)], refs[len(which) :]
+    copies = []
+    for n, k in enumerate(which):
         cols = pl.ds(pl.multiple_of(head_at(FEATURE_FROM[k]) * 512, 512), 512)
-        o[...] = dot_f32(at_ref[...], w_ref[:, cols]).astype(jnp.bfloat16)
+        c = pltpu.make_async_copy(w_hbm.at[:, cols], w_ref.at[n], sems.at[n])
+        c.start()
+        copies.append(c)
+    for n, o in enumerate(out_refs):
+        copies[n].wait()
+        o[...] = dot_f32(at_ref[...], w_ref[n]).astype(jnp.bfloat16)
 
 
 def attention_kernel(list_ref, q_ref, *refs):
@@ -353,6 +360,7 @@
             pltpu.SemaphoreType.DMA((32,)),
         ],
         cost_estimate=pl.CostEstimate(flops=2 * 10**10, transcendentals=10**7, bytes_accessed=10**7),
+        compiler_params=pltpu.CompilerParams(vmem_limit_bytes=24 << 20),
         name="attend",
     )(lists, q, *gathered)
 
@@ -376,6 +384,7 @@
         out_specs=VMEM,
         scratch_shapes=[pltpu.VMEM((2, ROWS, 512), bf16)],
         cost_estimate=pl.CostEstimate(flops=10**9, transcendentals=0, bytes_accessed=6 * 10**6),
+        compiler_params=pltpu.CompilerParams(vmem_limit_bytes=20 << 20),
         name="keys_values",
     )(gain, cosine, sine, *pieces, w_key, w_value)
     gathered = gather_blocks(kv)
@@ -389,6 +398,7 @@
         out_specs=[VMEM, SMEM],
         scratch_shapes=[pltpu.VMEM((2, ROWS, 512), bf16)],
         cost_estimate=pl.CostEstimate(flops=4 * 10**9, transcendentals=0, bytes_accessed=10**7),
+        compiler_params=pltpu.CompilerParams(vmem_limit_bytes=24 << 20),
         name="queries",
     )
     q, lists = query_call(gain, dilation, widths, cosine, sine, *pieces, w_query)
@@ -398,18 +408,22 @@
         return pl.pallas_call(
             functools.partial(out_kernel, which),
             out_shape=[jax.ShapeDtypeStruct((ROWS, 512), bf16)] * len(which),
-            in_specs=[VMEM, VMEM],
+            in_specs=[VMEM, ANY],
             out_specs=[VMEM] * len(which),
+            scratch_shapes=[
+                pltpu.VMEM((len(which), 512, 512), bf16),
+                pltpu.SemaphoreType.DMA((len(which),)),
+            ],
             cost_estimate=pl.CostEstimate(
                 flops=len(which) * 2**28, transcendentals=0, bytes_accessed=len(which) * 2**20
             ),
+            compiler_params=pltpu.CompilerParams(vmem_limit_bytes=16 << 20),
             name="project_out",
         )(attention, w_output)
 
-    first = (7, 4, 5)
-    second = (6, 1, 2, 3, 0)
-    part = dict(zip(first, shares(first)))
-    part.update(zip(second, shares(second)))
+    part = {}
+    for which in ((7,), (4, 5), (6, 1, 2, 3, 0)):
+        part.update(zip(which, shares(which)))
     return scatter_sums([part[k] for k in range(8)], tokens)
 
 

time: 190 us -> 184 us (0.968)
  the two profiles are of different devices: /device:TPU:6 before, /device:TPU:2 now
where the time goes in v2:
time: 184 us
  waiting for transfers between devices  93.1 us (51%)
  starting transfers between devices  36.8 us (20%)
  Pallas kernels  36.7 us (20%)
  local copies, waits for them, and re-layouts  10.3 us (6%)
  other arithmetic  6.39 us (3%)
    ppermute x25, waiting for transfers between devices, moved(): return lax.ppermute(x, axis, [(k, (k + step) % size) for k in range(size)])  58 us
    ppermute x6, waiting for transfers between devices, ring(): return lax.ppermute(x, ('seq_1', 'seq_2'), pairs)  35.1 us
    ppermute x25, starting transfers between devices, moved(): return lax.ppermute(x, axis, [(k, (k + step) % size) for k in range(size)])  34.6 us
    pallas_call x1, Pallas kernels, local_attention(): pl.pallas_call(attention_kernel, out_shape=jax.ShapeDtypeStruct((ROWS, 51...  23.4 us
    unnamed x66, local copies, waits for them, and re-layouts  9.42 us
    pallas_call x1, Pallas kernels, shards(): query_call(gain, dilation, widths, cosine, sine, *pieces, w_query)  5.31 us
    pallas_call x3, Pallas kernels, shares(): pl.pallas_call(functools.partial(out_kernel, which), out_shape=[jax.Shape...  4.2 us
    pallas_call x1, Pallas kernels, shards(): pl.pallas_call(kv_kernel, out_shape=jax.ShapeDtypeStruct((ROWS, 256), bf1...  3.77 us
  transfers between devices with their start and end apart: 31, of which 20 were waited for; matrix products, arithmetic and copies ran while one was open for 3% of the time, Pallas kernels for 5%

profile of v2, /device:TPU:2, one launch (start us, length us, event | category | flops | bytes accessed | tf_op | source)
XLA Modules:
  0.0 183.8 jit_solution(3986158881384773204)
XLA Ops:
  0.0 3.0 %collective-permute-start.2 = (bf16[512,512]{1,0:T(8,128)(2,1)}, bf16[512,512]{1,0:T(8,128)(2,1)S(1)}, u32[]{:S(2)}, u32[]{:S(2)}) collective-permute-start(bf16[512,512]{1,0:T(8,128)(2,1)} %refs_0_.3), channel_id=1, source_target_pairs={{0,6},{2,0},{4,2},{6,4},{1,7},{3,1},{5,3},{7,5},{8,14},{10,8},{12,... | collective-permute-start | bytes 1572872 | tf_op jit(solution)/shard_map/ppermute | solution.py:30
  5.1 9.4 %collective-permute-done.2.refs_3_ = bf16[512,512]{1,0:T(8,128)(2,1)S(1)} collective-permute-done((bf16[512,512]{1,0:T(8,128)(2,1)}, bf16[512,512]{1,0:T(8,128)(2,1)S(1)}, u32[]{:S(2)}, u32[]{:S(2)}) %collective-permute-start.2) | collective-permute-done | bytes 524320 | tf_op jit(solution)/shard_map/ppermute | solution.py:30
  14.5 3.7 %collective-permute-start.6 = (bf16[256,512]{1,0:T(8,128)(2,1)S(1)}, bf16[256,512]{1,0:T(8,128)(2,1)S(1)}, u32[]{:S(2)}, u32[]{:S(2)}) collective-permute-start(bf16[256,512]{1,0:T(8,128)(2,1)S(1)} %slice.37), channel_id=1, source_target_pairs={{0,6},{2,0},{4,2},{6,4},{1,7},{3,1},{5,3},{7,5},{8,14},{10,8},{12,... | collective-permute-start | bytes 786440 | tf_op jit(solution)/shard_map/ppermute | solution.py:30
  18.3 3.2 %collective-permute-start.4 = (bf16[512,512]{1,0:T(8,128)(2,1)S(1)}, bf16[512,512]{1,0:T(8,128)(2,1)S(1)}, u32[]{:S(2)}, u32[]{:S(2)}) collective-permute-start(bf16[512,512]{1,0:T(8,128)(2,1)S(1)} %collective-permute-done.refs_1_), channel_id=1, source_target_pairs={{0,6},{2,0},{4,2},{6,4},{1,7},{3,1},{5,3},{7,5},{8,14},{10,8},{12,... | collective-permute-start | bytes 1572872 | tf_op jit(solution)/shard_map/ppermute | solution.py:30
  22.3 2.6 %collective-permute-done.6.refs_7_ = bf16[256,512]{1,0:T(8,128)(2,1)S(1)} collective-permute-done((bf16[256,512]{1,0:T(8,128)(2,1)S(1)}, bf16[256,512]{1,0:T(8,128)(2,1)S(1)}, u32[]{:S(2)}, u32[]{:S(2)}) %collective-permute-start.6) | collective-permute-done | bytes 262176 | tf_op jit(solution)/shard_map/ppermute | solution.py:30
  34.3 2.8 %collective-permute-done.7.refs_8_ = bf16[256,512]{1,0:T(8,128)(2,1)S(1)} collective-permute-done((bf16[256,512]{1,0:T(8,128)(2,1)}, bf16[256,512]{1,0:T(8,128)(2,1)S(1)}, u32[]{:S(2)}, u32[]{:S(2)}) %collective-permute-start.7) | collective-permute-done | bytes 262176 | tf_op jit(solution)/shard_map/ppermute | solution.py:30
  39.0 3.8 %keys_values.1 = bf16[512,256]{1,0:T(8,128)(2,1)S(1)} custom-call(f32[8,512]{1,0:T(8,128)S(1)} %reshape.14.gain_ref, f32[512,128]{1,0:T(8,128)S(1)} %get-tuple-element.28.cos_ref, f32[512,128]{1,0:T(8,128)S(1)} %get-tuple-element.29.sin_ref, bf16[512,512]{1,0:T(8,128)(2,1)S(1)} %copy-done.1, bf16[512,512]{1,0:T(8,128)(2,1)S(1)} %collective-permute-done.refs_1_, ...), custom_call_target="tpu_custom_call" | custom-call | flops 1000000000 | bytes 6000000 | tf_op jit(solution)/shard_map/keys_values/pallas_call | solution.py:380
  47.8 11.1 %collective-permute-done.12.refs_2_ = bf16[1024,256]{1,0:T(8,128)(2,1)S(1)} collective-permute-done((bf16[1024,256]{1,0:T(8,128)(2,1)S(1)}, bf16[1024,256]{1,0:T(8,128)(2,1)S(1)}, u32[]{:S(2)}, u32[]{:S(2)}) %collective-permute-start.12) | collective-permute-done | bytes 524320 | tf_op jit(solution)/shard_map/ppermute | solution.py:75
  59.4 7.7 %collective-permute-done.10 = bf16[512,256]{1,0:T(8,128)(2,1)S(1)} collective-permute-done((bf16[512,256]{1,0:T(8,128)(2,1)S(1)}, bf16[512,256]{1,0:T(8,128)(2,1)S(1)}, u32[]{:S(2)}, u32[]{:S(2)}) %collective-permute-start.10) | collective-permute-done | bytes 262176 | tf_op jit(solution)/shard_map/ppermute | solution.py:30
  70.3 9.4 %collective-permute-done.15.refs_5_ = bf16[1024,256]{1,0:T(8,128)(2,1)S(1)} collective-permute-done((bf16[1024,256]{1,0:T(8,128)(2,1)S(1)}, bf16[1024,256]{1,0:T(8,128)(2,1)S(1)}, u32[]{:S(2)}, u32[]{:S(2)}) %collective-permute-start.15) | collective-permute-done | bytes 524320 | tf_op jit(solution)/shard_map/ppermute | solution.py:75
  79.8 5.5 %collective-permute-done.14.refs_4_ = bf16[1024,256]{1,0:T(8,128)(2,1)S(1)} collective-permute-done((bf16[1024,256]{1,0:T(8,128)(2,1)S(1)}, bf16[1024,256]{1,0:T(8,128)(2,1)S(1)}, u32[]{:S(2)}, u32[]{:S(2)}) %collective-permute-start.14) | collective-permute-done | bytes 524320 | tf_op jit(solution)/shard_map/ppermute | solution.py:75
  89.8 5.9 %collective-permute-done.17.refs_7_ = bf16[1024,256]{1,0:T(8,128)(2,1)S(1)} collective-permute-done((bf16[1024,256]{1,0:T(8,128)(2,1)S(1)}, bf16[1024,256]{1,0:T(8,128)(2,1)S(1)}, u32[]{:S(2)}, u32[]{:S(2)}) %collective-permute-start.17) | collective-permute-done | bytes 524320 | tf_op jit(solution)/shard_map/ppermute | solution.py:75
  95.7 8.7 %collective-permute-done.19.refs_9_ = bf16[512,256]{1,0:T(8,128)(2,1)S(1)} collective-permute-done((bf16[512,256]{1,0:T(8,128)(2,1)S(1)}, bf16[512,256]{1,0:T(8,128)(2,1)S(1)}, u32[]{:S(2)}, u32[]{:S(2)}) %collective-permute-start.19) | collective-permute-done | bytes 262176 | tf_op jit(solution)/shard_map/ppermute | solution.py:30
  112.6 5.3 %queries.1 = (bf16[512,512]{1,0:T(8,128)(2,1)S(1)}, s32[4,64]{1,0:T(4,128)S(1)}) custom-call(f32[8,512]{1,0:T(8,128)S(1)} %reshape.14.gain_ref, s32[128,8]{1,0:T(8,128)S(1)} %copy.9.dil_ref, s32[4]{0:T(128)S(1)} %copy-done.30, f32[512,128]{1,0:T(8,128)S(1)} %get-tuple-element.28.cos_ref, f32[512,128]{1,0:T(8,128)S(1)} %get-tuple-element.29.sin_ref, ...), custom_call_target="tpu_custom_call" | custom-call | flops 4000000000 | bytes 10000000 | tf_op jit(solution)/shard_map/queries/pallas_call | solution.py:404
  118.1 23.4 %attend.1.at_ref = bf16[512,512]{1,0:T(8,128)(2,1)S(1)} custom-call(s32[4,64]{1,0:T(4,128)S(1)} %get-tuple-element.14.list_ref, bf16[512,512]{1,0:T(8,128)(2,1)S(1)} %get-tuple-element.15.q_ref, bf16[1024,256]{1,0:T(8,128)(2,1)S(1)} %copy-done.14, bf16[1024,256]{1,0:T(8,128)(2,1)S(1)} %copy-done.28, bf16[1024,256]{1,0:T(8,128)(2,1)S(1)} %copy-done.16, ...), custom_call_target="tpu_custom_call" | custom-call | flops 20000000000 | bytes 10000000 | tf_op jit(solution)/shard_map/attend/pallas_call | solution.py:351
  145.4 3.3 %collective-permute-start.24 = (bf16[512,512]{1,0:T(8,128)(2,1)S(1)}, bf16[512,512]{1,0:T(8,128)(2,1)S(1)}, u32[]{:S(2)}, u32[]{:S(2)}) collective-permute-start(bf16[512,512]{1,0:T(8,128)(2,1)S(1)} %get-tuple-element.19), channel_id=1, source_target_pairs={{0,6},{2,0},{4,2},{6,4},{1,7},{3,1},{5,3},{7,5},{8,14},{10,8},{12,... | collective-permute-start | bytes 1572872 | tf_op jit(solution)/shard_map/ppermute | solution.py:30
  148.7 2.6 %project_out.3 = (bf16[512,512]{1,0:T(8,128)(2,1)S(1)}, bf16[512,512]{1,0:T(8,128)(2,1)S(1)}, bf16[512,512]{1,0:T(8,128)(2,1)S(1)}, bf16[512,512]{1,0:T(8,128)(2,1)S(1)}, bf16[512,512]{1,0:T(8,128)(2,1)S(1)}) custom-call(bf16[512,512]{1,0:T(8,128)(2,1)S(1)} %attend.1.at_ref, bf16[512,4096]{1,0:T(8,128)(2,1)S(1)} %copy-done), custom_call_target="tpu_custom_call" | custom-call | flops 1342177280 | bytes 5242880 | tf_op jit(solution)/shard_map/project_out/pallas_call | solution.py:408
  151.4 6.2 %collective-permute-done.26 = bf16[512,512]{1,0:T(8,128)(2,1)S(1)} collective-permute-done((bf16[512,512]{1,0:T(8,128)(2,1)S(1)}, bf16[512,512]{1,0:T(8,128)(2,1)S(1)}, u32[]{:S(2)}, u32[]{:S(2)}) %collective-permute-start.26) | collective-permute-done | bytes 524320 | tf_op jit(solution)/shard_map/ppermute | solution.py:30
  157.8 3.2 %collective-permute-start.29 = (bf16[256,512]{1,0:T(8,128)(2,1)S(1)}, bf16[256,512]{1,0:T(8,128)(2,1)S(1)}, u32[]{:S(2)}, u32[]{:S(2)}) collective-permute-start(bf16[256,512]{1,0:T(8,128)(2,1)S(1)} %get-tuple-element.24), channel_id=1, source_target_pairs={{0,6},{2,0},{4,2},{6,4},{1,7},{3,1},{5,3},{7,5},{8,14},{10,8},{12,... | collective-permute-start | bytes 786440 | tf_op jit(solution)/shard_map/ppermute | solution.py:30
  163.4 2.3 %collective-permute-done.29 = bf16[256,512]{1,0:T(8,128)(2,1)S(1)} collective-permute-done((bf16[256,512]{1,0:T(8,128)(2,1)S(1)}, bf16[256,512]{1,0:T(8,128)(2,1)S(1)}, u32[]{:S(2)}, u32[]{:S(2)}) %collective-permute-start.29) | collective-permute-done | bytes 262176 | tf_op jit(solution)/shard_map/ppermute | solution.py:30
  165.8 3.8 %collective-permute-start.30 = (bf16[512,512]{1,0:T(8,128)(2,1)S(1)}, bf16[512,512]{1,0:T(8,128)(2,1)S(1)}, u32[]{:S(2)}, u32[]{:S(2)}) collective-permute-start(bf16[512,512]{1,0:T(8,128)(2,1)S(1)} %pad_maximum_fusion.5), channel_id=1, source_target_pairs={{0,6},{2,0},{4,2},{6,4},{1,7},{3,1},{5,3},{7,5},{8,14},{10,8},{12,... | collective-permute-start | bytes 1572872 | tf_op jit(solution)/shard_map/ppermute | solution.py:30
  169.8 5.5 %collective-permute-done.25 = bf16[512,512]{1,0:T(8,128)(2,1)S(1)} collective-permute-done((bf16[512,512]{1,0:T(8,128)(2,1)S(1)}, bf16[512,512]{1,0:T(8,128)(2,1)S(1)}, u32[]{:S(2)}, u32[]{:S(2)}) %collective-permute-start.25) | collective-permute-done | bytes 524320 | tf_op jit(solution)/shard_map/ppermute | solution.py:30
  175.3 3.7 %collective-permute-done.30 = bf16[512,512]{1,0:T(8,128)(2,1)S(1)} collective-permute-done((bf16[512,512]{1,0:T(8,128)(2,1)S(1)}, bf16[512,512]{1,0:T(8,128)(2,1)S(1)}, u32[]{:S(2)}, u32[]{:S(2)}) %collective-permute-start.30) | collective-permute-done | bytes 524320 | tf_op jit(solution)/shard_map/ppermute | solution.py:30
  179.1 3.6 %collective-permute-done.28 = bf16[512,512]{1,0:T(8,128)(2,1)S(1)} collective-permute-done((bf16[512,512]{1,0:T(8,128)(2,1)S(1)}, bf16[512,512]{1,0:T(8,128)(2,1)S(1)}, u32[]{:S(2)}, u32[]{:S(2)}) %collective-permute-start.28) | collective-permute-done | bytes 524320 | tf_op jit(solution)/shard_map/ppermute | solution.py:30
  (133 shorter events, 43.7 us)
Async XLA Ops:
  0.0 14.5 %collective-permute-start.2 = (bf16[512,512]{1,0:T(8,128)(2,1)}, bf16[512,512]{1,0:T(8,128)(2,1)S(1)}, u32[]{:S(2)}, u32[]{:S(2)}) collective-permute-start(bf16[512,512]{1,0:T(8,128)(2,1)} %refs_0_.3), channel_id=1, source_target_pairs={{0,6},{2,0},{4,2},{6,4},{1,7},{3,1},{5,3},{7,5},{8,14},{10,8},{12,... | collective-permute-start | bytes 1572872 | tf_op jit(solution)/shard_map/ppermute | solution.py:30
  3.0 15.2 %collective-permute-start.1 = (bf16[512,512]{1,0:T(8,128)(2,1)}, bf16[512,512]{1,0:T(8,128)(2,1)S(1)}, u32[]{:S(2)}, u32[]{:S(2)}) collective-permute-start(bf16[512,512]{1,0:T(8,128)(2,1)} %refs_0_.3), channel_id=1, source_target_pairs={{0,2},{2,4},{4,6},{6,0},{1,3},{3,5},{5,7},{7,1},{8,10},{10,12},{12... | collective-permute-start | bytes 1572872 | tf_op jit(solution)/shard_map/ppermute | solution.py:30
  3.0 15.3 %collective-permute-start = (bf16[512,512]{1,0:T(8,128)(2,1)}, bf16[512,512]{1,0:T(8,128)(2,1)S(1)}, u32[]{:S(2)}, u32[]{:S(2)}) collective-permute-start(bf16[512,512]{1,0:T(8,128)(2,1)} %refs_0_.3), channel_id=1, source_target_pairs={{0,1},{1,0},{2,3},{3,2},{4,5},{5,4},{6,7},{7,6},{8,9},{9,8},{10,11... | collective-permute-start | bytes 1572872 | tf_op jit(solution)/shard_map/ppermute | solution.py:30
  14.5 10.4 %collective-permute-start.6 = (bf16[256,512]{1,0:T(8,128)(2,1)S(1)}, bf16[256,512]{1,0:T(8,128)(2,1)S(1)}, u32[]{:S(2)}, u32[]{:S(2)}) collective-permute-start(bf16[256,512]{1,0:T(8,128)(2,1)S(1)} %slice.37), channel_id=1, source_target_pairs={{0,6},{2,0},{4,2},{6,4},{1,7},{3,1},{5,3},{7,5},{8,14},{10,8},{12,... | collective-permute-start | bytes 786440 | tf_op jit(solution)/shard_map/ppermute | solution.py:30
  18.2 10.6 %collective-permute-start.5 = (bf16[256,512]{1,0:T(8,128)(2,1)S(1)}, bf16[256,512]{1,0:T(8,128)(2,1)}, u32[]{:S(2)}, u32[]{:S(2)}) collective-permute-start(bf16[256,512]{1,0:T(8,128)(2,1)S(1)} %slice.36), channel_id=1, source_target_pairs={{0,2},{2,4},{4,6},{6,0},{1,3},{3,5},{5,7},{7,1},{8,10},{10,12},{12... | collective-permute-start | bytes 786440 | tf_op jit(solution)/shard_map/ppermute | solution.py:30
  18.3 18.8 %collective-permute-start.4 = (bf16[512,512]{1,0:T(8,128)(2,1)S(1)}, bf16[512,512]{1,0:T(8,128)(2,1)S(1)}, u32[]{:S(2)}, u32[]{:S(2)}) collective-permute-start(bf16[512,512]{1,0:T(8,128)(2,1)S(1)} %collective-permute-done.refs_1_), channel_id=1, source_target_pairs={{0,6},{2,0},{4,2},{6,4},{1,7},{3,1},{5,3},{7,5},{8,14},{10,8},{12,... | collective-permute-start | bytes 1572872 | tf_op jit(solution)/shard_map/ppermute | solution.py:30
  21.5 16.4 %collective-permute-start.3 = (bf16[512,512]{1,0:T(8,128)(2,1)S(1)}, bf16[512,512]{1,0:T(8,128)(2,1)}, u32[]{:S(2)}, u32[]{:S(2)}) collective-permute-start(bf16[512,512]{1,0:T(8,128)(2,1)S(1)} %collective-permute-done.refs_1_), channel_id=1, source_target_pairs={{0,2},{2,4},{4,6},{6,0},{1,3},{3,5},{5,7},{7,1},{8,10},{10,12},{12... | collective-permute-start | bytes 1572872 | tf_op jit(solution)/shard_map/ppermute | solution.py:30
  45.8 13.1 %collective-permute-start.12 = (bf16[1024,256]{1,0:T(8,128)(2,1)S(1)}, bf16[1024,256]{1,0:T(8,128)(2,1)S(1)}, u32[]{:S(2)}, u32[]{:S(2)}) collective-permute-start(bf16[1024,256]{1,0:T(8,128)(2,1)S(1)} %pad_maximum_fusion.3.refs_0_), channel_id=1, source_target_pairs={{0,16},{8,120},{16,32},{24,8},{32,48},{40,24},{48,64},{56,40},{64,... | collective-permute-start | bytes 1572872 | tf_op jit(solution)/shard_map/ppermute | solution.py:75
  58.9 10.4 %collective-permute-start.13 = (bf16[1024,256]{1,0:T(8,128)(2,1)S(1)}, bf16[1024,256]{1,0:T(8,128)(2,1)S(1)}, u32[]{:S(2)}, u32[]{:S(2)}) collective-permute-start(bf16[1024,256]{1,0:T(8,128)(2,1)S(1)} %collective-permute-done.12.refs_2_), channel_id=1, source_target_pairs={{0,16},{8,120},{16,32},{24,8},{32,48},{40,24},{48,64},{56,40},{64,... | collective-permute-start | bytes 1572872 | tf_op jit(solution)/shard_map/ppermute | solution.py:75
  69.3 10.4 %collective-permute-start.15 = (bf16[1024,256]{1,0:T(8,128)(2,1)S(1)}, bf16[1024,256]{1,0:T(8,128)(2,1)S(1)}, u32[]{:S(2)}, u32[]{:S(2)}) collective-permute-start(bf16[1024,256]{1,0:T(8,128)(2,1)S(1)} %collective-permute-done.13.refs_3_), channel_id=1, source_target_pairs={{0,16},{8,120},{16,32},{24,8},{32,48},{40,24},{48,64},{56,40},{64,... | collective-permute-start | bytes 1572872 | tf_op jit(solution)/shard_map/ppermute | solution.py:75
  69.3 15.9 %collective-permute-start.14 = (bf16[1024,256]{1,0:T(8,128)(2,1)S(1)}, bf16[1024,256]{1,0:T(8,128)(2,1)S(1)}, u32[]{:S(2)}, u32[]{:S(2)}) collective-permute-start(bf16[1024,256]{1,0:T(8,128)(2,1)S(1)} %constant_dynamic-update-slice_fusion.refs_1_), channel_id=1, source_target_pairs={{0,16},{8,120},{16,32},{24,8},{32,48},{40,24},{48,64},{56,40},{64,... | collective-permute-start | bytes 1572872 | tf_op jit(solution)/shard_map/ppermute | solution.py:75
  85.3 10.4 %collective-permute-start.17 = (bf16[1024,256]{1,0:T(8,128)(2,1)S(1)}, bf16[1024,256]{1,0:T(8,128)(2,1)S(1)}, u32[]{:S(2)}, u32[]{:S(2)}) collective-permute-start(bf16[1024,256]{1,0:T(8,128)(2,1)S(1)} %collective-permute-done.14.refs_4_), channel_id=1, source_target_pairs={{0,16},{8,120},{16,32},{24,8},{32,48},{40,24},{48,64},{56,40},{64,... | collective-permute-start | bytes 1572872 | tf_op jit(solution)/shard_map/ppermute | solution.py:75
  85.3 19.1 %collective-permute-start.18 = (bf16[1024,256]{1,0:T(8,128)(2,1)S(1)}, bf16[1024,256]{1,0:T(8,128)(2,1)S(1)}, u32[]{:S(2)}, u32[]{:S(2)}) collective-permute-start(bf16[1024,256]{1,0:T(8,128)(2,1)S(1)} %collective-permute-done.15.refs_5_), channel_id=1, source_target_pairs={{0,128},{128,0},{1,129},{129,1},{2,130},{130,2},{3,131},{131,3},{4... | collective-permute-start | bytes 1572872 | tf_op jit(solution)/shard_map/ppermute | solution.py:30
  88.1 16.3 %collective-permute-start.19 = (bf16[512,256]{1,0:T(8,128)(2,1)S(1)}, bf16[512,256]{1,0:T(8,128)(2,1)S(1)}, u32[]{:S(2)}, u32[]{:S(2)}) collective-permute-start(bf16[512,256]{1,0:T(8,128)(2,1)S(1)} %collective-permute-done.16.refs_6_), channel_id=1, source_target_pairs={{0,128},{128,0},{1,129},{129,1},{2,130},{130,2},{3,131},{131,3},{4... | collective-permute-start | bytes 786440 | tf_op jit(solution)/shard_map/ppermute | solution.py:30
  89.8 28.2 %collective-permute-start.21 = (bf16[2560,256]{1,0:T(8,128)(2,1)}, bf16[2560,256]{1,0:T(8,128)(2,1)}, u32[]{:S(2)}, u32[]{:S(2)}) collective-permute-start(bf16[2560,256]{1,0:T(8,128)(2,1)} %pad_maximum_fusion), channel_id=1, source_target_pairs={{0,8},{8,0},{1,9},{9,1},{2,10},{10,2},{3,11},{11,3},{4,12},{12,4},... | collective-permute-start | bytes 3932168 | tf_op jit(solution)/shard_map/ppermute | solution.py:30
  105.6 12.3 %collective-permute-start.22 = (bf16[2560,256]{1,0:T(8,128)(2,1)}, bf16[2560,256]{1,0:T(8,128)(2,1)}, u32[]{:S(2)}, u32[]{:S(2)}) collective-permute-start(bf16[2560,256]{1,0:T(8,128)(2,1)} %pad_maximum_fusion.1), channel_id=1, source_target_pairs={{0,8},{8,0},{1,9},{9,1},{2,10},{10,2},{3,11},{11,3},{4,12},{12,4},... | collective-permute-start | bytes 3932168 | tf_op jit(solution)/shard_map/ppermute | solution.py:30
  106.7 11.2 %collective-permute-start.20 = (bf16[2048,256]{1,0:T(8,128)(2,1)}, bf16[2048,256]{1,0:T(8,128)(2,1)}, u32[]{:S(2)}, u32[]{:S(2)}) collective-permute-start(bf16[2048,256]{1,0:T(8,128)(2,1)} %pad_maximum_fusion.2), channel_id=1, source_target_pairs={{0,8},{8,0},{1,9},{9,1},{2,10},{10,2},{3,11},{11,3},{4,12},{12,4},... | collective-permute-start | bytes 3145736 | tf_op jit(solution)/shard_map/ppermute | solution.py:30
  142.1 15.4 %collective-permute-start.26 = (bf16[512,512]{1,0:T(8,128)(2,1)S(1)}, bf16[512,512]{1,0:T(8,128)(2,1)S(1)}, u32[]{:S(2)}, u32[]{:S(2)}) collective-permute-start(bf16[512,512]{1,0:T(8,128)(2,1)S(1)} %project_out.5), channel_id=1, source_target_pairs={{0,1},{1,0},{2,3},{3,2},{4,5},{5,4},{6,7},{7,6},{8,9},{9,8},{10,11... | collective-permute-start | bytes 1572872 | tf_op jit(solution)/shard_map/ppermute | solution.py:30
  145.3 15.7 %collective-permute-start.23 = (bf16[512,512]{1,0:T(8,128)(2,1)S(1)}, bf16[512,512]{1,0:T(8,128)(2,1)S(1)}, u32[]{:S(2)}, u32[]{:S(2)}) collective-permute-start(bf16[512,512]{1,0:T(8,128)(2,1)S(1)} %get-tuple-element.18), channel_id=1, source_target_pairs={{0,2},{2,4},{4,6},{6,0},{1,3},{3,5},{5,7},{7,1},{8,10},{10,12},{12... | collective-permute-start | bytes 1572872 | tf_op jit(solution)/shard_map/ppermute | solution.py:30
  145.4 15.6 %collective-permute-start.24 = (bf16[512,512]{1,0:T(8,128)(2,1)S(1)}, bf16[512,512]{1,0:T(8,128)(2,1)S(1)}, u32[]{:S(2)}, u32[]{:S(2)}) collective-permute-start(bf16[512,512]{1,0:T(8,128)(2,1)S(1)} %get-tuple-element.19), channel_id=1, source_target_pairs={{0,6},{2,0},{4,2},{6,4},{1,7},{3,1},{5,3},{7,5},{8,14},{10,8},{12,... | collective-permute-start | bytes 1572872 | tf_op jit(solution)/shard_map/ppermute | solution.py:30
  157.7 11.9 %collective-permute-start.27 = (bf16[256,512]{1,0:T(8,128)(2,1)S(1)}, bf16[256,512]{1,0:T(8,128)(2,1)S(1)}, u32[]{:S(2)}, u32[]{:S(2)}) collective-permute-start(bf16[256,512]{1,0:T(8,128)(2,1)S(1)} %get-tuple-element.23), channel_id=1, source_target_pairs={{0,2},{2,4},{4,6},{6,0},{1,3},{3,5},{5,7},{7,1},{8,10},{10,12},{12... | collective-permute-start | bytes 786440 | tf_op jit(solution)/shard_map/ppermute | solution.py:30
  161.2 14.1 %collective-permute-start.25 = (bf16[512,512]{1,0:T(8,128)(2,1)S(1)}, bf16[512,512]{1,0:T(8,128)(2,1)S(1)}, u32[]{:S(2)}, u32[]{:S(2)}) collective-permute-start(bf16[512,512]{1,0:T(8,128)(2,1)S(1)} %add_convert_fusion.2), channel_id=1, source_target_pairs={{0,1},{1,0},{2,3},{3,2},{4,5},{5,4},{6,7},{7,6},{8,9},{9,8},{10,11... | collective-permute-start | bytes 1572872 | tf_op jit(solution)/shard_map/ppermute | solution.py:30
  165.8 13.2 %collective-permute-start.30 = (bf16[512,512]{1,0:T(8,128)(2,1)S(1)}, bf16[512,512]{1,0:T(8,128)(2,1)S(1)}, u32[]{:S(2)}, u32[]{:S(2)}) collective-permute-start(bf16[512,512]{1,0:T(8,128)(2,1)S(1)} %pad_maximum_fusion.5), channel_id=1, source_target_pairs={{0,6},{2,0},{4,2},{6,4},{1,7},{3,1},{5,3},{7,5},{8,14},{10,8},{12,... | collective-permute-start | bytes 1572872 | tf_op jit(solution)/shard_map/ppermute | solution.py:30
  169.7 13.0 %collective-permute-start.28 = (bf16[512,512]{1,0:T(8,128)(2,1)S(1)}, bf16[512,512]{1,0:T(8,128)(2,1)S(1)}, u32[]{:S(2)}, u32[]{:S(2)}) collective-permute-start(bf16[512,512]{1,0:T(8,128)(2,1)S(1)} %pad_maximum_fusion.4), channel_id=1, source_target_pairs={{0,2},{2,4},{4,6},{6,0},{1,3},{3,5},{5,7},{7,1},{8,10},{10,12},{12... | collective-permute-start | bytes 1572872 | tf_op jit(solution)/shard_map/ppermute | solution.py:30
  (39 other events, 408.4 us)
